TPU v7x, 128 devices: a whole 4x4x4 slice. The times are simulated.
128 devices in a mesh: cell: 2 (over core), panel: 2 (over x_lo), sc: 32 (over z, y, x_hi).
Axes of the slice: x: 4 (x_hi: 2, x_lo: 2; x = x_hi * 2 + x_lo), y: 4, z: 4, core: 2. Of those that a mesh axis runs over, the one named last changes fastest.
Arguments:
- channel: bfloat16 [4, 1024, 2, 1024, 128], P('cell', 'sc', None, 'panel'), may hold values from -0.1875 to 0.1875
- received: bfloat16 [4, 1024, 2, 14, 1024], P('cell', 'sc', None, None, 'panel'), may hold values from -6 to 6
- noise_power: float32 [4], P('cell'), may hold values from 0.05 to 0.5
- user_count: int32 [4, 64], P('cell', 'sc'), may hold values from 32 to 128
- serving_cell: int32 [4, 128, 1], P('cell'), may hold values from 0 to 3; in each aligned block of 256 rows (0 to 255, 256 to 511, ..., all dimensions but the last counted through in order) at most 128 rows name the same one
Outputs:
- routed_symbols: bfloat16 [4, 256, 2, 14, 1024], P('cell', 'sc')
Inputs may be any that keep to these rules, and one draw needn't show every extreme that they name: `serving_cell`: at most 128 user slots of one block of 2 consecutive cells name the same serving cell, and in every draw some serving cell is named exactly 128 times by one block.
All inputs are finite; a program needn't handle non-finite values.
Results may differ from a plain program's by a relative error of at most 0.0057.
Values may be sent and summed in bfloat16 or wider, within the bound.
A program may use at most 128 MiB of HBM per device.

v0:
```python
import jax
import jax.numpy as jnp
from jax import lax
from jax.sharding import PartitionSpec as P

GRP = 16
ITERS = 2


def with_halo(block, sides, width):
    for axis, dim in sides:
        count = lax.axis_size(axis)
        forward = [(i, i + 1) for i in range(count - 1)]
        backward = [(target, source) for source, target in forward]
        low = lax.ppermute(
            lax.slice_in_dim(block, block.shape[dim] - width, None, axis=dim), axis, forward
        )
        high = lax.ppermute(lax.slice_in_dim(block, 0, width, axis=dim), axis, backward)
        block = jnp.concatenate([low, block, high], axis=dim)
    return block


def adjoint_apply(matrix, vector):
    products = jnp.einsum("cfaku,cfbsk->cfabsu", matrix, vector, preferred_element_type=jnp.float32)
    return jnp.stack(
        (products[:, :, 0, 0] + products[:, :, 1, 1], products[:, :, 0, 1] - products[:, :, 1, 0]),
        axis=2,
    )


def apply_channel(matrix, vector):
    products = jnp.einsum("cfaku,cfbsu->cfabsk", matrix, vector, preferred_element_type=jnp.float32)
    return jnp.stack(
        (products[:, :, 0, 0] - products[:, :, 1, 1], products[:, :, 0, 1] + products[:, :, 1, 0]),
        axis=2,
    )


def user_sum(left, right):
    return jnp.sum(left * right, axis=(2, 4))


def widen(values):
    return values[:, :, None, :, None]


def body(channel, received, noise_power, user_count, serving_cell):
    cells, band, _, antennas, users = channel.shape
    padded = with_halo(channel, (("sc", 1),), 1)
    total = band * lax.axis_size("sc")
    index = lax.axis_index("sc") * band + lax.iota(jnp.int32, band)
    weight = jnp.where((index == 0) | (index == total - 1), 0.75, 1.0).astype(jnp.float32)
    lower = padded[:, :-2].astype(jnp.float32)
    middle = padded[:, 1:-1].astype(jnp.float32)
    upper = padded[:, 2:].astype(jnp.float32)
    smooth = (0.25 * lower + 0.5 * middle + 0.25 * upper) / weight[None, :, None, None, None]
    counts = jnp.repeat(user_count, GRP, axis=1)
    active = (lax.iota(jnp.int32, users)[None, None, :] < counts[:, :, None]).astype(jnp.float32)
    smoothed = (smooth * active[:, :, None, None, :]).astype(jnp.bfloat16)
    partial_sums = adjoint_apply(smoothed, received)
    noise = noise_power[:, None, None, None, None]
    matched = lax.psum(partial_sums, "panel")
    estimate = jnp.zeros_like(matched)
    residual = matched
    direction = matched
    norm_now = user_sum(residual, residual)
    for iteration in range(ITERS):
        column_image = apply_channel(smoothed, direction.astype(jnp.bfloat16)).astype(jnp.bfloat16)
        image = lax.psum(adjoint_apply(smoothed, column_image), "panel") + noise * direction
        alpha = norm_now / user_sum(direction, image)
        estimate = estimate + widen(alpha) * direction
        residual = residual - widen(alpha) * image
        norm_next = user_sum(residual, residual)
        direction = residual + widen(norm_next / norm_now) * direction
        norm_now = norm_next
    detected = estimate.astype(jnp.bfloat16)
    n_cell = lax.axis_size("cell")
    capacity = 2 * users // n_cell
    slot_count = n_cell * capacity
    keys = serving_cell[:, :, 0].reshape(-1)
    position = lax.iota(jnp.int32, cells * users)
    earlier = (keys[:, None] == keys[None, :]) & (position[None, :] < position[:, None])
    rank = jnp.sum(earlier.astype(jnp.int32), axis=1)
    target = keys % cells * slot_count + keys // cells * capacity + rank
    onehot = (target[:, None] == lax.iota(jnp.int32, cells * slot_count)[None, :]).astype(
        jnp.bfloat16
    )
    onehot = onehot.reshape(cells, users, cells * slot_count)
    outgoing = jnp.einsum("cfasu,cut->tasf", detected, onehot, preferred_element_type=jnp.float32)
    outgoing = outgoing.astype(jnp.bfloat16).reshape(cells, slot_count, 2, detected.shape[3], band)
    return lax.all_to_all(
        lax.all_to_all(outgoing, "cell", split_axis=1, concat_axis=1, tiled=True),
        "sc",
        split_axis=1,
        concat_axis=4,
        tiled=True,
    )


def solution(mesh):
    return jax.shard_map(
        body,
        mesh=mesh,
        in_specs=(
            P("cell", "sc", None, "panel", None),
            P("cell", "sc", None, None, "panel"),
            P("cell"),
            P("cell", "sc"),
            P("cell", None, None),
        ),
        out_specs=P("cell", "sc", None, None, None),
        check_vma=False,
    )
```

profile of v0, /device:TPU:1, one launch (start us, length us, event | category | flops | bytes accessed | tf_op | source)
XLA Modules:
  0.0 358.5 jit_solution(6481282010595207241)
XLA Ops:
  6.5 2.2 fusion.48
  8.7 5.5 %collective-permute-start = (bf16[2,1,2,512,128]{4,3,2,1,0:T(8,128)(2,1)}, bf16[2,1,2,512,128]{4,3,2,1,0:T(8,128)(2,1)S(1)}, u32[]{:S(2)}, u32[]{:S(2)}) collective-permute-start(bf16[2,1,2,512,128]{4,3,2,1,0:T(8,128)(2,1)} %get-tuple-element.7), channel_id=1, source_target_pairs={{0,1},{1,2},{2,3},{3,4},{4,5},{5,6},{6,7},{7,8},{8,9},{9,10},{10,1... | collective-permute-start | bytes 1572872 | tf_op jit(solution)/shard_map/ppermute | solution.py:15
  14.2 1.3 collective-permute-start.1
  15.5 0.8 broadcast_in_dim.12
  16.5 8.7 %collective-permute-done = bf16[2,1,2,512,128]{4,3,2,1,0:T(8,128)(2,1)S(1)} collective-permute-done((bf16[2,1,2,512,128]{4,3,2,1,0:T(8,128)(2,1)}, bf16[2,1,2,512,128]{4,3,2,1,0:T(8,128)(2,1)S(1)}, u32[]{:S(2)}, u32[]{:S(2)}) %collective-permute-start) | collective-permute-done | bytes 524320 | tf_op jit(solution)/shard_map/ppermute | solution.py:15
  25.1 13.1 %collective-permute-done.1 = bf16[2,1,2,512,128]{4,3,2,1,0:T(8,128)(2,1)S(1)} collective-permute-done((bf16[2,1,2,512,128]{4,3,2,1,0:T(8,128)(2,1)S(1)}, bf16[2,1,2,512,128]{4,3,2,1,0:T(8,128)(2,1)S(1)}, u32[]{:S(2)}, u32[]{:S(2)}) %collective-permute-start.1) | collective-permute-done | bytes 524320 | tf_op jit(solution)/shard_map/ppermute | solution.py:18
  38.2 26.0 %multiply_convert_fusion = bf16[2,32,2,512,128]{4,3,2,1,0:T(8,128)(2,1)} fusion(bf16[2,32,2,512,128]{4,3,2,1,0:T(8,128)(2,1)} %param.5, bf16[2,1,2,512,128]{4,3,2,1,0:T(8,128)(2,1)S(1)} %collective-permute-done.1, bf16[2,1,2,512,128]{4,3,2,1,0:T(8,128)(2,1)S(1)} %collective-permute-done, f32[2,32,128]{2,1,0:T(8,128)S(1)} %fusion.44, f32[32]{0:T(128)S(1)} %or_select_fusion), kind=kLoop, calls=%fused_computation | loop fusion | flops 109051904 | bytes 34635904 | tf_op jit(solution)/shard_map/convert_element_type | solution.py:59
  64.2 7.0 %fusion = f32[2,32,2,128,2,14]{3,5,4,2,1,0:T(8,128)S(1)} fusion(bf16[2,32,2,512,128]{4,3,2,1,0:T(8,128)(2,1)} %multiply_convert_fusion, bf16[2,32,2,14,512,1]{4,2,3,1,0,5:T(2,128)(2,1)S(1)} %bitcast.138), kind=kOutput, calls=%fused_computation.3 | convolution fusion | flops 469762048 | bytes 20447232 | tf_op jit(solution)/shard_map/cfaku,cfbsk->cfabsu/dot_general | solution.py:24
  71.2 1.1 copy.169
  72.3 0.2 fusion.39
  72.5 1.0 pad_maximum_fusion.2
  73.5 0.2 all-reduce.6.cloned.1.call-start
  73.7 46.5 %all-reduce.4.cloned.1.call-done = f32[2,32,2,14,128]{4,1,3,2,0:T(8,128)} async-done(((f32[2,32,2,14,128]{4,1,3,2,0:T(8,128)}), f32[2,32,2,14,128]{4,1,3,2,0:T(8,128)}) %all-reduce.4.cloned.1.call-update) | async-done | bytes 917520 | tf_op jit(solution)/shard_map/psum | solution.py:62
  120.2 1.3 convert_bitcast_fusion.1
  121.5 14.8 %fusion.10 = f32[2,32,2,2,14,512]{5,4,2,3,1,0:T(8,128)} fusion(bf16[2,32,2,512,128]{4,3,2,1,0:T(8,128)(2,1)} %multiply_convert_fusion, bf16[2,32,2,14,128,1]{4,1,3,2,0,5:T(8,128)(2,1)S(1)} %convert_bitcast_fusion.1), kind=kOutput, calls=%fused_computation.14 | convolution fusion | flops 469762048 | bytes 24576000 | tf_op jit(solution)/shard_map/cfaku,cfbsu->cfabsk/dot_general | solution.py:32
  136.3 2.6 fusion.26
  139.0 2.6 fusion.27
  141.6 8.2 %fusion.6 = f32[2,32,2,14,2,128]{5,3,4,2,1,0:T(8,128)S(1)} fusion(bf16[2,32,2,512,128]{4,3,2,1,0:T(8,128)(2,1)} %multiply_convert_fusion, bf16[2,32,1,14,512]{4,3,1,0,2:T(8,128)(2,1)S(1)} %fusion.27, bf16[2,32,1,14,512]{4,3,1,0,2:T(8,128)(2,1)S(1)} %fusion.26), kind=kOutput, calls=%fused_computation.9 | convolution fusion | flops 470679552 | bytes 20447232 | tf_op jit(solution)/shard_map/cfaku,cfbsk->cfabsu/dot_general | solution.py:24
  149.8 1.1 copy.168
  150.9 0.2 fusion.37
  151.1 1.0 pad_maximum_fusion.3
  152.1 0.3 all-reduce.8.cloned.1.call-start
  152.3 44.6 %all-reduce.6.cloned.1.call-done = f32[2,32,2,14,128]{4,1,3,2,0:T(8,128)} async-done(((f32[2,32,2,14,128]{4,1,3,2,0:T(8,128)}), f32[2,32,2,14,128]{4,1,3,2,0:T(8,128)}) %all-reduce.6.cloned.1.call-update) | async-done | bytes 917520 | tf_op jit(solution)/shard_map/psum | solution.py:69
  197.0 1.7 multiply_reduce_fusion.2
  198.7 1.6 multiply_reduce_fusion.1
  200.3 0.4 convert_bitcast_fusion
  200.7 14.8 %fusion.13 = f32[2,32,2,2,14,512]{5,4,2,3,1,0:T(8,128)} fusion(bf16[2,32,2,512,128]{4,3,2,1,0:T(8,128)(2,1)} %multiply_convert_fusion, bf16[2,32,2,14,128,1]{4,1,3,2,0,5:T(8,128)(2,1)S(1)} %convert_bitcast_fusion), kind=kOutput, calls=%fused_computation.15 | convolution fusion | flops 469762048 | bytes 24576000 | tf_op jit(solution)/shard_map/cfaku,cfbsu->cfabsk/dot_general | solution.py:32
  215.6 2.6 fusion.28
  218.2 2.6 fusion.29
  220.8 8.2 %fusion.2 = f32[2,32,2,14,2,128]{5,3,4,2,1,0:T(8,128)S(1)} fusion(bf16[2,32,2,512,128]{4,3,2,1,0:T(8,128)(2,1)} %multiply_convert_fusion, bf16[2,32,1,14,512]{4,3,1,0,2:T(8,128)(2,1)S(1)} %fusion.29, bf16[2,32,1,14,512]{4,3,1,0,2:T(8,128)(2,1)S(1)} %fusion.28), kind=kOutput, calls=%fused_computation.5 | convolution fusion | flops 470679552 | bytes 20447232 | tf_op jit(solution)/shard_map/cfaku,cfbsk->cfabsu/dot_general | solution.py:24
  229.0 1.1 copy.167
  230.3 1.0 pad_maximum_fusion.4
  231.3 0.2 convert_reduce_fusion
  231.5 44.7 %all-reduce.8.cloned.1.call-done = f32[2,32,2,14,128]{4,1,3,2,0:T(8,128)} async-done(((f32[2,32,2,14,128]{4,1,3,2,0:T(8,128)}), f32[2,32,2,14,128]{4,1,3,2,0:T(8,128)}) %all-reduce.8.cloned.1.call-update) | async-done | bytes 917520 | tf_op jit(solution)/shard_map/psum | solution.py:69
  276.2 1.7 multiply_reduce_fusion
  277.9 0.7 fusion.25
  278.7 0.2 reshape.282
  278.9 7.0 %copy.123 = bf16[2,256,2,14,32]{4,2,3,0,1:T(2,128)(2,1)} copy(bf16[2,256,2,14,32]{1,0,4,3,2:T(2,128)(2,1)S(1)} %reshape.282) | data formatting | bytes 1835008 | tf_op jit(solution)/shard_map/reshape | solution.py:90
  285.9 5.1 %reshape.292 = bf16[2,2,114688]{2,1,0:T(2,128)(2,1)S(1)} reshape(bf16[256,2,14,2,32]{4,3,2,1,0:T(2,128)(2,1)} %bitcast.141) | data formatting | bytes 1835008
  291.0 5.1 %all_to_all.23 = bf16[2,2,114688]{2,1,0:T(2,128)(2,1)S(1)} all-to-all(bf16[2,2,114688]{2,1,0:T(2,128)(2,1)S(1)} %reshape.292), channel_id=1, replica_groups=mesh['cell'=2,'panel'=2,'sc'=32] {'cell'}, dimensions={0} | all-to-all | bytes 1835008 | tf_op jit(solution)/shard_map/all_to_all | solution.py:92
  296.1 3.0 reshape.293
  299.1 6.3 %bitcast_bitcast_fusion = bf16[256,2,14,2,32]{4,3,2,1,0:T(2,128)(2,1)} fusion(bf16[256,2,14,2,32]{4,3,2,1,0:T(2,128)(2,1)} %reshape.293), kind=kLoop, calls=%fused_computation.89 | loop fusion | bytes 1835008
  305.4 5.0 %reshape.294 = bf16[32,2,7168]{2,1,0:T(2,128)(2,1)S(1)} reshape(bf16[256,2,14,2,32]{4,3,2,1,0:T(2,128)(2,1)} %bitcast_bitcast_fusion) | data formatting | bytes 1835008
  310.4 26.1 %all_to_all.24 = bf16[32,2,7168]{2,1,0:T(2,128)(2,1)S(1)} all-to-all(bf16[32,2,7168]{2,1,0:T(2,128)(2,1)S(1)} %reshape.294), channel_id=1, replica_groups=mesh['cell'=2,'panel'=2,'sc'=32] {'sc'}, dimensions={0} | all-to-all | bytes 1835008 | tf_op jit(solution)/shard_map/all_to_all | solution.py:91
  336.5 3.2 reshape.295
  339.8 2.9 copy.166
  342.7 2.8 copy.146
  345.5 6.5 %reshape.291 = bf16[2,8,2,14,1024]{4,2,3,1,0:T(2,128)(2,1)} reshape(bf16[2,8,2,14,32,32]{5,4,2,3,1,0:T(8,128)(2,1)} %copy.146) | data formatting | bytes 1835008 | tf_op jit(solution)/shard_map/all_to_all | solution.py:91
  (24 shorter events, 0.5 us)
Async XLA Ops:
  6.5 57.7 %copy-start = (bf16[2,32,2,14,512]{4,2,3,1,0:T(2,128)(2,1)S(1)}, bf16[2,32,2,14,512]{4,2,3,1,0:T(2,128)(2,1)}, u32[]{:S(2)}) copy-start(bf16[2,32,2,14,512]{4,2,3,1,0:T(2,128)(2,1)} %param.6) | copy-start | bytes 5505028
  6.5 113.7 %all-reduce.4.cloned.1.call-start = ((), (), s32[]{:S(2)}) async-start(), calls=%async_computation.2 | async-start | bytes 1835008 | tf_op jit(solution)/shard_map/psum | solution.py:62
  8.7 16.4 %collective-permute-start = (bf16[2,1,2,512,128]{4,3,2,1,0:T(8,128)(2,1)}, bf16[2,1,2,512,128]{4,3,2,1,0:T(8,128)(2,1)S(1)}, u32[]{:S(2)}, u32[]{:S(2)}) collective-permute-start(bf16[2,1,2,512,128]{4,3,2,1,0:T(8,128)(2,1)} %get-tuple-element.7), channel_id=1, source_target_pairs={{0,1},{1,2},{2,3},{3,4},{4,5},{5,6},{6,7},{7,8},{8,9},{9,10},{10,1... | collective-permute-start | bytes 1572872 | tf_op jit(solution)/shard_map/ppermute | solution.py:15
  14.2 24.0 %collective-permute-start.1 = (bf16[2,1,2,512,128]{4,3,2,1,0:T(8,128)(2,1)S(1)}, bf16[2,1,2,512,128]{4,3,2,1,0:T(8,128)(2,1)S(1)}, u32[]{:S(2)}, u32[]{:S(2)}) collective-permute-start(bf16[2,1,2,512,128]{4,3,2,1,0:T(8,128)(2,1)S(1)} %get-tuple-element.8), channel_id=1, source_target_pairs={{1,0},{2,1},{3,2},{4,3},{5,4},{6,5},{7,6},{8,7},{9,8},{10,9},{11,1... | collective-permute-start | bytes 1572872 | tf_op jit(solution)/shard_map/ppermute | solution.py:18
  73.5 123.5 %all-reduce.6.cloned.1.call-start = ((), (), s32[]{:S(2)}) async-start(), calls=%async_computation.3 | async-start | bytes 1835008 | tf_op jit(solution)/shard_map/psum | solution.py:69
  150.8 46.1 %copy-start.2 = (f32[2,32,2,14,128]{4,1,3,2,0:T(8,128)S(1)}, f32[2,32,2,14,128]{4,1,3,2,0:T(8,128)}, u32[]{:S(2)}) copy-start(f32[2,32,2,14,128]{4,1,3,2,0:T(8,128)} %all-reduce.4.cloned.1.call-done) | copy-start | bytes 2752516
  150.9 46.1 %copy-start.5 = (f32[2]{0:T(128)S(1)}, f32[2]{0:T(128)}, u32[]{:S(2)}) copy-start(f32[2]{0:T(128)} %param.7) | copy-start | bytes 28
  152.1 124.1 %all-reduce.8.cloned.1.call-start = ((), (), s32[]{:S(2)}) async-start(), calls=%async_computation.4 | async-start | bytes 1835008 | tf_op jit(solution)/shard_map/psum | solution.py:69
  197.0 3.3 copy-start.3
  230.1 1.2 copy-start.4
  342.7 9.3 %copy-start.1 = (bf16[2,32,2,14,512]{4,2,3,1,0:T(2,128)(2,1)S(1)}, bf16[2,32,2,14,512]{4,2,3,1,0:T(2,128)(2,1)}, u32[]{:S(2)}) copy-start(bf16[2,32,2,14,512]{4,2,3,1,0:T(2,128)(2,1)} %param.6) | copy-start | bytes 5505028
Sparse Core Ops, SparseCore 0:
  73.6 46.5 all-reduce.3
  152.2 44.7 all-reduce.5
  231.4 44.7 all-reduce.7
where the time goes:
time: 360 us; the launch traced here: 359 us
  waiting for transfers between devices  158 us (44%)
  matrix products  53.8 us (15%)
  local copies, waits for them, and re-layouts  48.4 us (13%)
  other arithmetic  46.9 us (13%)
  blocking collectives  31.2 us (9%)
  between operations  13.4 us (4%)
  starting transfers between devices  7.26 us (2%)
    psum x2, waiting for transfers between devices, body(): lax.psum(adjoint_apply(smoothed, column_image), 'panel') + noise * direction  89.4 us
    psum x1, waiting for transfers between devices, body(): matched = lax.psum(partial_sums, 'panel')  46.5 us
    dot_general x2, matrix products, apply_channel(): jnp.einsum('cfaku,cfbsu->cfabsk', matrix, vector, preferred_element_type=...  29.7 us
    all_to_all x1, blocking collectives, body(): lax.all_to_all(lax.all_to_all(outgoing, 'cell', split_axis=1, concat_axis...  26.1 us
    convert_element_type x1, other arithmetic, body(): smoothed = (smooth * active[:, :, None, None, :]).astype(jnp.bfloat16)  26 us
    dot_general x3, matrix products, adjoint_apply(): jnp.einsum('cfaku,cfbsk->cfabsu', matrix, vector, preferred_element_type=...  23.4 us
    unnamed x17, local copies, waits for them, and re-layouts  22.7 us
    ppermute x1, waiting for transfers between devices, with_halo(): lax.ppermute(lax.slice_in_dim(block, 0, width, axis=dim), axis, backward)  13.1 us
  transfers between devices with their start and end apart: 5, of which 5 were waited for; matrix products, arithmetic and copies ran while one was open for 0% of the time, Pallas kernels for 0%

commit v1 on v0

v1 whole, which is shorter than its diff:
```python
import functools

import jax
import jax.numpy as jnp
from jax import lax
from jax.experimental import pallas as pl
from jax.experimental.pallas import tpu as pltpu
from jax.sharding import PartitionSpec as P

GRP = 16
MESH = pl.DeviceIdType.MESH
F32, BF16 = jnp.float32, jnp.bfloat16

BAND, ANT, USERS, SYM = 32, 512, 128, 14
INNER = BAND - 2
SIZE = 10
PER_CELL = INNER // SIZE
GROUPS = 2 * PER_CELL
UNITS = 2 * BAND


def adjoint(rows, block):
    out = jnp.dot(rows, block, preferred_element_type=F32)
    real = out[:16, :128] + out[16:, 128:]
    imag = out[16:, :128] - out[:16, 128:]
    return real, imag


def forward(real, imag, block):
    left = jnp.concatenate(
        [jnp.concatenate([real, -imag], axis=1), jnp.concatenate([imag, real], axis=1)], axis=0
    )
    return lax.dot_general(left, block, (((1,), (1,)), ((), ())), preferred_element_type=F32)


def row_sum(values):
    return jnp.sum(values, axis=1, keepdims=True)


def detect_kernel(
    channel, received, noise, counts, keys, out,
    raw, smooth, rx, halo, msend, mrecv, isend, irecv, qsend, qrecv, norm1, dirsq, first, second, det,
    raw_sem, rx_sem, halo_ssem, halo_rsem, m_ssem, m_rsem, i_ssem, i_rsem, q_ssem, q_rsem,
):
    c_id, p_id, s_id = lax.axis_index("cell"), lax.axis_index("panel"), lax.axis_index("sc")
    n_sc = lax.axis_size("sc")
    partner = (c_id, 1 - p_id, s_id)
    upper = (c_id, p_id, lax.rem(s_id + 1, n_sc))
    lower = (c_id, p_id, lax.rem(s_id + n_sc - 1, n_sc))

    def raw_copy(c, k):
        rows = pl.ds(k * SIZE + 2, SIZE)
        return pltpu.make_async_copy(channel.at[c, rows], raw.at[c, rows], raw_sem.at[c, k])

    def head_copy(c):
        rows = pl.ds(0, 2)
        return pltpu.make_async_copy(channel.at[c, rows], raw.at[c, rows], raw_sem.at[c, PER_CELL])

    def rx_copy(c):
        return pltpu.make_async_copy(
            received.at[c], rx.at[c], rx_sem.at[c]
        )

    for c in range(2):
        head_copy(c).start()
        rx_copy(c).start()
        for k in range(PER_CELL):
            raw_copy(c, k).start()

    barrier = pltpu.get_barrier_semaphore()
    for device in (partner, upper, lower):
        pl.semaphore_signal(barrier, inc=1, device_id=device, device_id_type=MESH)
    pl.semaphore_wait(barrier, 3)

    halo_copies = []
    for c in range(2):
        for side, (edge, device) in enumerate(((BAND - 1, upper), (0, lower))):
            halo_copies.append(
                pltpu.make_async_remote_copy(
                    src_ref=channel.at[c, edge],
                    dst_ref=halo.at[c, side],
                    send_sem=halo_ssem.at[c, side],
                    recv_sem=halo_rsem.at[c, side],
                    device_id=device,
                    device_id_type=MESH,
                )
            )
    for copy in halo_copies:
        copy.start()

    def exchange(source, target, ssem, rsem, start, size, slot):
        return pltpu.make_async_remote_copy(
            src_ref=source.at[pl.ds(start, size)],
            dst_ref=target.at[pl.ds(start, size)],
            send_sem=ssem.at[slot],
            recv_sem=rsem.at[slot],
            device_id=partner,
            device_id_type=MESH,
        )

    def group_copy(pair, g):
        source, target, ssem, rsem = pair
        return exchange(source, target, ssem, rsem, g * SIZE, SIZE, g)

    def edge_copy(pair):
        source, target, ssem, rsem = pair
        return exchange(source, target, ssem, rsem, GROUPS * SIZE, 4, GROUPS)

    m_pair = (msend, mrecv, m_ssem, m_rsem)
    i_pair = (isend, irecv, i_ssem, i_rsem)
    lane = lax.broadcasted_iota(jnp.int32, (16, 128), 1)

    def mask_of(c, f):
        return lane < counts[c, f // GRP]

    STRIP = 64

    def smooth_block(n, low, mid, high, low_gain, high_gain):
        for part in range(2):
            for row in range(0, ANT, STRIP):
                rows = pl.ds(row, STRIP)
                a = low[part, rows, :].astype(F32)
                b = mid[part, rows, :].astype(F32)
                d = high[part, rows, :].astype(F32)
                if low_gain is not None:
                    a = a * low_gain
                if high_gain is not None:
                    d = d * high_gain
                smooth[n, rows, pl.ds(128 * part, 128)] = (a + d + (b + b)).astype(BF16)

    def matched_terms(n, c, f, gain):
        real, imag = adjoint(rx[c, f].reshape(32, ANT), smooth[n])
        msend[n, 0] = (real * gain).astype(BF16)
        msend[n, 1] = (imag * gain).astype(BF16)

    def matched(n):
        real = msend[n, 0].astype(F32) + mrecv[n, 0].astype(F32)
        imag = msend[n, 1].astype(F32) + mrecv[n, 1].astype(F32)
        return real, imag

    def image_terms(n, c, f, gain):
        keep = mask_of(c, f)
        real, imag = matched(n)
        real, imag = jnp.where(keep, real, 0.0), jnp.where(keep, imag, 0.0)
        column = forward(real.astype(BF16), imag.astype(BF16), smooth[n])
        column = (column * gain).astype(BF16)
        real, imag = adjoint(column, smooth[n])
        isend[n, 0] = (real * gain).astype(BF16)
        isend[n, 1] = (imag * gain).astype(BF16)

    def second_terms(n, c, f, gain):
        keep = mask_of(c, f)
        power = noise[c]
        br, bi = matched(n)
        br, bi = jnp.where(keep, br, 0.0), jnp.where(keep, bi, 0.0)
        ir = isend[n, 0].astype(F32) + irecv[n, 0].astype(F32)
        ii = isend[n, 1].astype(F32) + irecv[n, 1].astype(F32)
        ir = jnp.where(keep, ir, 0.0) + power * br
        ii = jnp.where(keep, ii, 0.0) + power * bi
        norm0 = row_sum(br * br + bi * bi)
        alpha = norm0 / row_sum(br * ir + bi * ii)
        er, ei = alpha * br, alpha * bi
        rr, ri = br - alpha * ir, bi - alpha * ii
        norm = row_sum(rr * rr + ri * ri)
        beta = norm / norm0
        dr, di = rr + beta * br, ri + beta * bi
        first[n, 0], first[n, 1] = er, ei
        second[n, 0], second[n, 1] = dr, di
        column = forward(dr.astype(BF16), di.astype(BF16), smooth[n]) * gain
        square = column * column
        square = square[:16] + square[16:]
        square = (square[:, :128] + square[:, 128:256]) + (square[:, 256:384] + square[:, 384:])
        here = lane == n
        qsend[...] = jnp.where(here, row_sum(square), qsend[...])
        norm1[...] = jnp.where(here, norm, norm1[...])
        dirsq[...] = jnp.where(here, power * row_sum(dr * dr + di * di), dirsq[...])

    low_end, high_end = s_id == 0, s_id == n_sc - 1
    edge_gain = (
        jnp.where(low_end, 1.0 / 3.0, 0.25).astype(F32),
        jnp.where(high_end, 1.0 / 3.0, 0.25).astype(F32),
    )
    halo_gain = (jnp.where(low_end, 0.0, 1.0).astype(F32), jnp.where(high_end, 0.0, 1.0).astype(F32))

    def each_inner(g, run, unroll):
        c = g // PER_CELL
        base = lax.rem(g, PER_CELL) * SIZE + 1

        def step(i, _):
            for k in range(unroll):
                run(g * SIZE + i * unroll + k, c, base + i * unroll + k, 0.25)
            return 0

        lax.fori_loop(0, SIZE // unroll, step, 0)

    def each_edge(run):
        def step(c, _):
            for side in range(2):
                run(GROUPS * SIZE + 2 * c + side, c, side * (BAND - 1), edge_gain[side])
            return 0

        lax.fori_loop(0, 2, step, 0)

    for c in range(2):
        head_copy(c).wait()
        rx_copy(c).wait()

    def first_unit(n, c, f, gain):
        smooth_block(n, raw.at[c, f - 1], raw.at[c, f], raw.at[c, f + 1], None, None)
        matched_terms(n, c, f, gain)

    def first_phase(g, _):
        raw_copy(g // PER_CELL, lax.rem(g, PER_CELL)).wait()
        each_inner(g, first_unit, 1)
        group_copy(m_pair, g).start()
        return 0

    lax.fori_loop(0, GROUPS, first_phase, 0)

    def image_phase(g, _):
        group_copy(m_pair, g).wait()
        each_inner(g, image_terms, 5)
        group_copy(i_pair, g).start()
        return 0

    def second_phase(g, _):
        group_copy(i_pair, g).wait()
        each_inner(g, second_terms, 5)
        return 0

    for copy in halo_copies:
        copy.wait()

    def edge_first(c, _):
        for side in range(2):
            n = GROUPS * SIZE + 2 * c + side
            f = side * (BAND - 1)
            if side == 0:
                smooth_block(n, halo.at[c, 0], raw.at[c, 0], raw.at[c, 1], halo_gain[0], None)
            else:
                smooth_block(n, raw.at[c, f - 1], raw.at[c, f], halo.at[c, 1], None, halo_gain[1])
            matched_terms(n, c, f, edge_gain[side])
        return 0

    lax.fori_loop(0, 2, edge_first, 0)
    edge_copy(m_pair).start()

    lax.fori_loop(0, GROUPS, image_phase, 0)
    edge_copy(m_pair).wait()
    each_edge(image_terms)
    edge_copy(i_pair).start()

    qsend[...] = jnp.zeros_like(qsend)
    norm1[...] = jnp.ones_like(norm1)
    dirsq[...] = jnp.ones_like(dirsq)
    lax.fori_loop(0, GROUPS, second_phase, 0)
    edge_copy(i_pair).wait()
    each_edge(second_terms)

    q_copy = pltpu.make_async_remote_copy(
        src_ref=qsend, dst_ref=qrecv, send_sem=q_ssem, recv_sem=q_rsem,
        device_id=partner, device_id_type=MESH,
    )
    q_copy.start()

    key = keys[...]
    users2 = 2 * USERS
    rows_i = lax.broadcasted_iota(jnp.int32, (users2, users2), 0)
    cols_i = lax.broadcasted_iota(jnp.int32, (users2, users2), 1)
    key_f = key.astype(F32)
    key_row = jnp.sum(jnp.where(rows_i == cols_i, key_f, 0.0), axis=0, keepdims=True)
    earlier = (key_f == key_row) & (rows_i < cols_i)
    rank_row = jnp.sum(jnp.where(earlier, 1.0, 0.0), axis=0, keepdims=True).astype(jnp.int32)
    key_row = key_row.astype(jnp.int32)
    place = (key_row // 2) * 256 + (rank_row // 8) * 16 + lax.rem(key_row, 2) * 8 + lax.rem(rank_row, 8)

    q_copy.wait()
    alpha1 = norm1[...] / (qsend[...] + qrecv[...] + dirsq[...])
    norm1[...] = alpha1

    def finish(n, c, f, gain):
        del gain
        alpha = row_sum(jnp.where(lane == n, norm1[...], 0.0))
        for part in range(2):
            value = first[n, part] + alpha * second[n, part]
            det[c, pl.ds(part * 512 + f, 16, stride=BAND), :] = value

    def finish_phase(g, _):
        each_inner(g, finish, 5)
        return 0

    lax.fori_loop(0, GROUPS, finish_phase, 0)
    each_edge(finish)

    half = SYM * BAND
    table = jnp.concatenate(
        [
            jnp.concatenate([det[c, pl.ds(0, half), :], det[c, pl.ds(512, half), :]], axis=0).astype(BF16)
            for c in range(2)
        ],
        axis=1,
    )
    for row in range(0, 512, 128):
        slot = lax.broadcasted_iota(jnp.int32, (128, users2), 0) + row
        onehot = jnp.where(slot == place, 1.0, 0.0).astype(BF16)
        sent = lax.dot_general(onehot, table, (((1,), (1,)), ((), ())), preferred_element_type=F32)
        out[pl.ds(row, 128), :] = sent.astype(BF16)


def deliver_kernel(outgoing, arrived, ssem, rsem, lsem):
    c_id, p_id, s_id = lax.axis_index("cell"), lax.axis_index("panel"), lax.axis_index("sc")
    n_sc = lax.axis_size("sc")
    half = n_sc // 2
    barrier = pltpu.get_barrier_semaphore()
    origin = s_id // half

    def panel_to(other):
        return jnp.where(lax.rem(other, 2) == lax.rem(s_id, 2), p_id, 1 - p_id)

    def from_self(j):
        return (origin == c_id) & (j == s_id)

    def to_self(k):
        return (k // half == c_id) & (c_id * half + lax.rem(k, half) == s_id)

    def greet(j, _):
        @pl.when(jnp.logical_not(from_self(j)))
        def _():
            pl.semaphore_signal(barrier, inc=1, device_id=(origin, panel_to(j), j), device_id_type=MESH)

        return 0

    lax.fori_loop(0, n_sc, greet, 0)
    own = origin == c_id
    pl.semaphore_wait(barrier, n_sc - jnp.where(own, 1, 0))

    def target(i):
        k = lax.rem(i + s_id, n_sc)
        return k, c_id * half + lax.rem(k, half)

    def remote(k, other):
        return pltpu.make_async_remote_copy(
            src_ref=outgoing.at[k], dst_ref=arrived.at[s_id], send_sem=ssem.at[k], recv_sem=rsem.at[s_id],
            device_id=(k // half, panel_to(other), other), device_id_type=MESH,
        )

    def local(k):
        return pltpu.make_async_copy(outgoing.at[k], arrived.at[s_id], lsem)

    def send(i, _):
        k, other = target(i)

        @pl.when(to_self(k))
        def _():
            local(k).start()

        @pl.when(jnp.logical_not(to_self(k)))
        def _():
            remote(k, other).start()

        return 0

    lax.fori_loop(0, n_sc, send, 0)

    def finish(i, _):
        k, other = target(i)

        @pl.when(to_self(k))
        def _():
            local(k).wait()

        @pl.when(jnp.logical_not(to_self(k)))
        def _():
            remote(k, other).wait_send()

        @pl.when(jnp.logical_not(from_self(i)))
        def _():
            pltpu.make_async_remote_copy(
                src_ref=outgoing.at[0], dst_ref=arrived.at[i], send_sem=ssem.at[0], recv_sem=rsem.at[i],
                device_id=(origin, panel_to(i), i), device_id_type=MESH,
            ).wait_recv()

        return 0

    lax.fori_loop(0, n_sc, finish, 0)


def assemble_kernel(arrived, out, rows):
    lane = lax.broadcasted_iota(jnp.int32, (16, 128), 1)
    for tile in range(7):
        blocks = [arrived[k, :, pl.ds(128 * tile, 128)].astype(F32) for k in range(4)]
        for m in range(4):
            value = blocks[m]
            for k in range(4):
                if k != m:
                    moved = pltpu.roll(blocks[k], (32 * (k - m)) % 128, 1)
                    inside = (lane >= 32 * k) & (lane < 32 * k + 32)
                    value = jnp.where(inside, moved, value)
            which = 4 * tile + m
            rows[pl.ds((which // SYM) * 16 + which % SYM, 16, stride=32), :] = value
    for slot in range(16):
        for part in range(2):
            out[slot, part] = rows[pl.ds(slot * 32 + part * 16, SYM), :].astype(BF16)


def body(channel, received, noise_power, user_count, serving_cell):
    vmem = pltpu.VMEM
    keys = serving_cell.reshape(2 * USERS, 1).astype(jnp.int32)
    received = jnp.pad(received, ((0, 0), (0, 0), (0, 0), (0, 2), (0, 0)))
    dma = pltpu.SemaphoreType.DMA
    outgoing = pl.pallas_call(
        detect_kernel,
        name="detect",
        out_shape=jax.ShapeDtypeStruct((512, 2 * SYM * BAND), BF16),
        in_specs=[
            pl.BlockSpec(memory_space=pl.ANY),
            pl.BlockSpec(memory_space=pl.ANY),
            pl.BlockSpec(memory_space=pltpu.SMEM),
            pl.BlockSpec(memory_space=pltpu.SMEM),
            pl.BlockSpec(memory_space=vmem),
        ],
        out_specs=pl.BlockSpec(memory_space=vmem),
        scratch_shapes=[
            vmem((2, BAND, 2, ANT, USERS), BF16),
            vmem((UNITS, ANT, 2 * USERS), BF16),
            vmem((2, BAND, 2, 16, ANT), BF16),
            vmem((2, 2, 2, ANT, USERS), BF16),
            vmem((UNITS, 2, 16, USERS), BF16),
            vmem((UNITS, 2, 16, USERS), BF16),
            vmem((UNITS, 2, 16, USERS), BF16),
            vmem((UNITS, 2, 16, USERS), BF16),
            vmem((16, 128), F32),
            vmem((16, 128), F32),
            vmem((16, 128), F32),
            vmem((16, 128), F32),
            vmem((UNITS, 2, 16, USERS), F32),
            vmem((UNITS, 2, 16, USERS), F32),
            vmem((2, 1024, USERS), F32),
            dma((2, PER_CELL + 1)),
            dma((2,)),
            dma((2, 2)),
            dma((2, 2)),
            dma((GROUPS + 1,)),
            dma((GROUPS + 1,)),
            dma((GROUPS + 1,)),
            dma((GROUPS + 1,)),
            dma,
            dma,
        ],
        compiler_params=pltpu.CompilerParams(
            collective_id=0, has_side_effects=True, vmem_limit_bytes=60 * 1024 * 1024
        ),
    )(channel, received, noise_power, user_count, keys)
    arrived = pl.pallas_call(
        deliver_kernel,
        name="deliver",
        out_shape=jax.ShapeDtypeStruct((BAND, 16, 2 * SYM * BAND), BF16),
        in_specs=[pl.BlockSpec(memory_space=pl.ANY)],
        out_specs=pl.BlockSpec(memory_space=pl.ANY),
        scratch_shapes=[dma((32,)), dma((32,)), dma],
        compiler_params=pltpu.CompilerParams(collective_id=1, has_side_effects=True),
    )(outgoing.reshape(32, 16, 2 * SYM * BAND))
    routed = pl.pallas_call(
        assemble_kernel,
        name="assemble",
        grid=(8,),
        out_shape=jax.ShapeDtypeStruct((16, 2, SYM, 32 * BAND), BF16),
        in_specs=[pl.BlockSpec((4, 16, 2 * SYM * BAND), lambda i: (i, 0, 0))],
        out_specs=pl.BlockSpec((16, 2, SYM, 128), lambda i: (0, 0, 0, i)),
        scratch_shapes=[vmem((512, 128), F32)],
    )(arrived)
    return routed.reshape(2, 8, 2, SYM, 32 * BAND)


def solution(mesh):
    return jax.shard_map(
        body,
        mesh=mesh,
        in_specs=(
            P("cell", "sc", None, "panel", None),
            P("cell", "sc", None, None, "panel"),
            P("cell"),
            P("cell", "sc"),
            P("cell", None, None),
        ),
        out_specs=P("cell", "sc", None, None, None),
        check_vma=False,
    )
```

time: 360 us -> 103 us (0.29)
  waiting for transfers between devices: 158 us -> 0 us
  Pallas kernels: 0 us -> 94.8 us
  matrix products: 53.8 us -> 0 us
  other arithmetic: 46.9 us -> 0 us
  local copies, waits for them, and re-layouts: 48.4 us -> 7.6 us
  blocking collectives: 31.2 us -> 0 us
  between operations: 13.4 us -> 0.03 us
  starting transfers between devices: 7.26 us -> 0 us
    psum x3 -> x0, waiting for transfers between devices: 136 us -> none  [the longest x2 89.4 us: body(): lax.psum(adjoint_apply(smoothed, column_image), 'panel') + noise * direction]
    pallas_call x0 -> x3, Pallas kernels: none -> 94.8 us  [the longest x1 65.8 us: body(): pl.pallas_call(detect_kernel, name='detect', out_shape=jax.ShapeDtypeStru...]
    dot_general x6 -> x0, matrix products: 53.8 us -> none  [the longest x2 29.7 us: apply_channel(): jnp.einsum('cfaku,cfbsu->cfabsk', matrix, vector, preferred_element_type=...]
    all_to_all x2 -> x0, blocking collectives: 31.2 us -> none  [the longest x1 26.1 us: body(): lax.all_to_all(lax.all_to_all(outgoing, 'cell', split_axis=1, concat_axis...]
    convert_element_type x4 -> x0, other arithmetic: 27.7 us -> none  [the longest x1 26 us: body(): smoothed = (smooth * active[:, :, None, None, :]).astype(jnp.bfloat16)]
    ppermute x2 -> x0, waiting for transfers between devices: 21.8 us -> none  [the longest x1 13.1 us: with_halo(): lax.ppermute(lax.slice_in_dim(block, 0, width, axis=dim), axis, backward)]
    unnamed x17 -> x3, local copies, waits for them, and re-layouts: 22.7 us -> 2 us
    all_to_all x3 -> x0, local copies, waits for them, and re-layouts: 12.2 us -> none  [body(): lax.all_to_all(lax.all_to_all(outgoing, 'cell', split_axis=1, concat_axis...]
  transfers between devices with their start and end apart: 5 -> 0, of which waited for: 5 -> 0; matrix products, arithmetic and copies ran while one was open for 0% -> 0% of each run, Pallas kernels for 0% -> 0%
where the time goes in v1:
time: 103 us; the launch traced here: 102 us
  Pallas kernels  94.8 us (92%)
  local copies, waits for them, and re-layouts  7.6 us (7%)
    pallas_call x1, Pallas kernels, body(): pl.pallas_call(detect_kernel, name='detect', out_shape=jax.ShapeDtypeStru...  65.8 us
    pallas_call x1, Pallas kernels, body(): pl.pallas_call(deliver_kernel, name='deliver', out_shape=jax.ShapeDtypeSt...  22.8 us
    pallas_call x1, Pallas kernels, body(): pl.pallas_call(assemble_kernel, name='assemble', grid=(8,), out_shape=jax...  6.25 us
    reshape x1, local copies, waits for them, and re-layouts, body(): return routed.reshape(2, 8, 2, SYM, 32 * BAND)  3.1 us

profile of v1, /device:TPU:1, one launch (start us, length us, event | category | flops | bytes accessed | tf_op | source)
XLA Modules:
  0.0 102.4 jit_solution(16381544455948559888)
XLA Ops:
  0.0 2.0 %copy.8 = bf16[2,32,2,14,512]{4,3,2,1,0:T(8,128)(2,1)S(1)} copy(bf16[2,32,2,14,512]{4,2,3,1,0:T(2,128)(2,1)} %param.6) | data formatting | bytes 3670016 | tf_op args[1]
  2.0 0.0 copy-start
  2.0 1.7 %pad.4.received = bf16[2,32,2,16,512]{4,3,2,1,0:T(8,128)(2,1)} pad(bf16[2,32,2,14,512]{4,3,2,1,0:T(8,128)(2,1)S(1)} %copy.8, bf16[]{:T(256)} %constant.2.clone.1), padding=0_0x0_0x0_0x0_2x0_0 | pad | bytes 3932162 | tf_op jit(solution)/shard_map/jit(_pad)/pad | solution.py:409
  3.7 0.0 copy-done
  3.7 0.8 copy.9.keys
  4.5 65.8 %detect.1 = bf16[512,896]{1,0:T(8,128)(2,1)} custom-call(bf16[2,32,2,512,128]{4,3,2,1,0:T(8,128)(2,1)} %channel.1, bf16[2,32,2,16,512]{4,3,2,1,0:T(8,128)(2,1)} %pad.4.received, f32[2]{0:T(128)} %noise.1, s32[2,2]{1,0:T(2,128)} %counts.1, s32[256,1]{1,0:T(8,128)} %copy.9.keys), custom_call_target="tpu_custom_call" | custom-call | tf_op jit(solution)/shard_map/detect/pallas_call | solution.py:411
  70.3 22.8 %deliver.1.arrived = bf16[32,16,896]{2,1,0:T(8,128)(2,1)} custom-call(bf16[32,16,896]{2,1,0:T(8,128)(2,1)} %bitcast.4), custom_call_target="tpu_custom_call" | custom-call | tf_op jit(solution)/shard_map/deliver/pallas_call | solution.py:454
  93.1 6.2 %assemble.1 = bf16[16,2,14,1024]{3,2,1,0:T(8,128)(2,1)} custom-call(bf16[32,16,896]{2,1,0:T(8,128)(2,1)} %deliver.1.arrived), custom_call_target="tpu_custom_call" | custom-call | tf_op jit(solution)/shard_map/assemble/pallas_call | solution.py:463
  99.3 3.1 %copy.10 = bf16[2,8,2,14,1024]{4,2,3,1,0:T(2,128)(2,1)} copy(bf16[2,8,2,14,1024]{4,3,2,1,0:T(8,128)(2,1)} %bitcast.3) | data formatting | bytes 1835008 | tf_op jit(solution)/shard_map/reshape | solution.py:472
Async XLA Ops:
  2.0 1.7 %copy-start = (s32[2,128,1]{1,2,0:T(1,128)S(1)}, s32[2,128,1]{1,2,0:T(1,128)}, u32[]{:S(2)}) copy-start(s32[2,128,1]{1,2,0:T(1,128)} %param.9) | copy-start | bytes 3076

commit v2 on v1

v2 whole, which is shorter than its diff:
```python
import functools

import jax
import jax.numpy as jnp
from jax import lax
from jax.experimental import pallas as pl
from jax.experimental.pallas import tpu as pltpu
from jax.sharding import PartitionSpec as P

GRP = 16
MESH = pl.DeviceIdType.MESH
F32, BF16 = jnp.float32, jnp.bfloat16

BAND, ANT, USERS, SYM = 32, 512, 128, 14
INNER = BAND - 2
SIZE = 10
PER_CELL = INNER // SIZE
GROUPS = 2 * PER_CELL
UNITS = 2 * BAND


def adjoint(rows, block):
    out = jnp.dot(rows, block, preferred_element_type=F32)
    real = out[:16, :128] + out[16:, 128:]
    imag = out[16:, :128] - out[:16, 128:]
    return real, imag


def forward(real, imag, block):
    left = jnp.concatenate(
        [jnp.concatenate([real, -imag], axis=1), jnp.concatenate([imag, real], axis=1)], axis=0
    )
    return lax.dot_general(left, block, (((1,), (1,)), ((), ())), preferred_element_type=F32)


def row_sum(values):
    return jnp.sum(values, axis=1, keepdims=True)


def detect_kernel(
    channel, received, noise, counts, keys, out,
    raw, smooth, rx, rx_other, split, halo, msend, mrecv, isend, irecv, xsend, xrecv, ysend, yrecv, own2,
    columns, qsend, qrecv, alphas, norm1, dirsq, first, second, det, onehot,
    raw_sem, rx_sem, halo_ssem, halo_rsem, o_ssem, o_rsem, m_ssem, m_rsem, i_ssem, i_rsem,
    x_ssem, x_rsem, q_ssem, q_rsem,
):
    c_id, p_id, s_id = lax.axis_index("cell"), lax.axis_index("panel"), lax.axis_index("sc")
    n_sc = lax.axis_size("sc")
    partner = (c_id, 1 - p_id, s_id)
    upper = (c_id, 1 - p_id, lax.rem(s_id + 1, n_sc))
    lower = (c_id, 1 - p_id, lax.rem(s_id + n_sc - 1, n_sc))
    edges = [(c, side, GROUPS * SIZE + 2 * c + side, side * (BAND - 1)) for c in range(2) for side in range(2)]

    def raw_copy(c, k):
        rows = pl.ds(k * SIZE + 2, SIZE)
        return pltpu.make_async_copy(channel.at[c, rows], raw.at[c, rows], raw_sem.at[c, k])

    def head_copy(c):
        rows = pl.ds(0, 2)
        return pltpu.make_async_copy(channel.at[c, rows], raw.at[c, rows], raw_sem.at[c, PER_CELL])

    def rx_copy(c):
        return pltpu.make_async_copy(received.at[c], rx.at[c, :, pl.ds(0, SYM)], rx_sem.at[c])

    for c in range(2):
        head_copy(c).start()
        rx_copy(c).start()
        for k in range(PER_CELL):
            raw_copy(c, k).start()

    barrier = pltpu.get_barrier_semaphore()
    for device in (partner, upper, lower):
        pl.semaphore_signal(barrier, inc=1, device_id=device, device_id_type=MESH)
    pl.semaphore_wait(barrier, 3)

    def remote(source, target, ssem, rsem, device):
        return pltpu.make_async_remote_copy(
            src_ref=source, dst_ref=target, send_sem=ssem, recv_sem=rsem,
            device_id=device, device_id_type=MESH,
        )

    other_copies = [
        remote(
            received.at[c, f], rx_other.at[c, side, pl.ds(0, SYM)],
            o_ssem.at[c, side], o_rsem.at[c, side], partner,
        )
        for c, side, n, f in edges
    ]
    halo_copies = [
        remote(
            channel.at[c, BAND - 1 - f, part], halo.at[c, side, :, pl.ds(128 * part, 128)],
            halo_ssem.at[c, side, part], halo_rsem.at[c, side, part], (upper, lower)[side],
        )
        for c, side, n, f in edges
        for part in range(2)
    ]
    for copy in halo_copies + other_copies:
        copy.start()

    def group_copy(pair, g):
        source, target, ssem, rsem = pair
        rows = pl.ds(g * SIZE, SIZE)
        return remote(source.at[rows], target.at[rows], ssem.at[g], rsem.at[g], partner)

    def edge_copy(pair):
        source, target, ssem, rsem = pair
        rows = pl.ds(GROUPS * SIZE, 4)
        return remote(source.at[rows], target.at[rows], ssem.at[GROUPS], rsem.at[GROUPS], partner)

    m_pair = (msend, mrecv, m_ssem, m_rsem)
    i_pair = (isend, irecv, i_ssem, i_rsem)
    x_copy = remote(xsend, xrecv, x_ssem.at[0], x_rsem.at[0], partner)
    y_copy = remote(ysend, yrecv, x_ssem.at[1], x_rsem.at[1], partner)
    lane = lax.broadcasted_iota(jnp.int32, (16, 128), 1)

    users2 = 2 * USERS
    key_row = jnp.concatenate([keys[0], keys[1]], axis=1).astype(F32)
    rows_i = lax.broadcasted_iota(jnp.int32, (users2, users2), 0)
    cols_i = lax.broadcasted_iota(jnp.int32, (users2, users2), 1)
    key_f = jnp.sum(jnp.where(rows_i == cols_i, key_row, 0.0), axis=1, keepdims=True)
    earlier = (key_f == key_row) & (rows_i < cols_i)
    rank_row = jnp.sum(jnp.where(earlier, 1.0, 0.0), axis=0, keepdims=True).astype(jnp.int32)
    key_row = key_row.astype(jnp.int32)
    place = (key_row // 2) * 256 + (rank_row // 8) * 16 + lax.rem(key_row, 2) * 8 + lax.rem(rank_row, 8)
    for row in range(0, 512, 64):
        slot = lax.broadcasted_iota(jnp.int32, (64, users2), 0) + row
        onehot[pl.ds(row, 64), :] = jnp.where(slot == place, 1.0, 0.0).astype(BF16)

    def spot(n):
        c = n // INNER
        return c, lax.rem(n, INNER) + 1

    def keep(values, c, f):
        mask = lane < counts[c, f // GRP]
        return [jnp.where(mask, v, 0.0) for v in values]

    def total(mine, theirs, n):
        pad = jnp.zeros((2, USERS), F32)
        return [
            jnp.concatenate([mine[n, a].astype(F32) + theirs[n, a].astype(F32), pad], axis=0)
            for a in range(2)
        ]

    def put(target, n, values, gain):
        for a in range(2):
            target[n, a] = (values[a][:SYM] * gain).astype(BF16)

    def sample_rows(block, k):
        both = block.reshape(32, ANT).astype(F32)
        for tile in range(ANT // 128):
            split[k, tile] = both[:, 128 * tile : 128 * tile + 128]
        return jnp.concatenate(
            [
                jnp.concatenate(
                    [split.at[k, tile][pl.ds(a, 16, stride=2), :] for tile in range(ANT // 128)], axis=1
                )
                for a in range(2)
            ],
            axis=0,
        ).astype(BF16)

    for c in range(2):
        head_copy(c).wait()
        rx_copy(c).wait()

    def first_phase(g, _):
        raw_copy(g // PER_CELL, lax.rem(g, PER_CELL)).wait()
        c = g // PER_CELL
        base = lax.rem(g, PER_CELL) * SIZE

        def strip(i, _):
            rows = pl.ds(pl.multiple_of(i * 32, 32), 32)
            for part in range(2):
                low, here = raw[c, base, part, rows, :], raw[c, base + 1, part, rows, :]
                for j in range(SIZE):
                    high = raw[c, base + j + 2, part, rows, :]
                    smooth[g * SIZE + j, rows, pl.ds(128 * part, 128)] = (low + high) + (here + here)
                    low, here = here, high
            return 0

        lax.fori_loop(0, ANT // 32, strip, 0)

        def match(i, _):
            for k in range(5):
                n = g * SIZE + 5 * i + k
                terms = adjoint(sample_rows(rx[c, base + 5 * i + k + 1], k), smooth[n])
                put(msend, n, terms, 0.25)
            return 0

        lax.fori_loop(0, SIZE // 5, match, 0)
        group_copy(m_pair, g).start()
        return 0

    lax.fori_loop(0, GROUPS, first_phase, 0)

    def edge_strip(i, _):
        rows = pl.ds(pl.multiple_of(i * 64, 64), 64)
        for c, side, n, f in edges:
            for part in range(2):
                here, inner = raw[c, f, part, rows, :], raw[c, 1 + side * (BAND - 3), part, rows, :]
                smooth[n, rows, pl.ds(128 * part, 128)] = inner + (here + here)
        return 0

    lax.fori_loop(0, ANT // 64, edge_strip, 0)

    def pipeline(low, high, begin, stage_a, stage_b, end):
        begin(low)
        stage_a(2 * low, 0)

        def step(g, _):
            stage_b(2 * g, 0)
            stage_a(2 * g + 1, 1)
            begin(g + 1)
            stage_b(2 * g + 1, 1)
            stage_a(2 * g + 2, 0)
            end(g)
            return 0

        lax.fori_loop(low, high - 1, step, 0)
        last = high - 1
        stage_b(2 * last, 0)
        stage_a(2 * last + 1, 1)
        stage_b(2 * last + 1, 1)
        end(last)

    def column_stage(batch, slot):
        for k in range(5):
            n = 5 * batch + k
            real, imag = keep(total(msend, mrecv, n), *spot(n))
            column = forward(real.astype(BF16), imag.astype(BF16), smooth[n])
            columns[slot, k] = (column * 0.25).astype(BF16)

    def image_stage(batch, slot):
        for k in range(5):
            n = 5 * batch + k
            put(isend, n, adjoint(columns[slot, k], smooth[n]), 0.25)

    def image_phase(low, high):
        pipeline(
            low, high, lambda g: group_copy(m_pair, g).wait(), column_stage, image_stage,
            lambda g: group_copy(i_pair, g).start(),
        )

    def step_terms(n, c, f):
        power = noise[c]
        br, bi = keep(total(msend, mrecv, n), c, f)
        ir, ii = keep(total(isend, irecv, n), c, f)
        ir, ii = ir + power * br, ii + power * bi
        norm0 = row_sum(br * br + bi * bi)
        alpha = norm0 / row_sum(br * ir + bi * ii)
        first[n, 0], first[n, 1] = alpha * br, alpha * bi
        rr, ri = br - alpha * ir, bi - alpha * ii
        norm = row_sum(rr * rr + ri * ri)
        beta = norm / norm0
        dr, di = rr + beta * br, ri + beta * bi
        second[n, 0], second[n, 1] = dr, di
        return norm, power * row_sum(dr * dr + di * di)

    def collect(target, pairs):
        value = target[...]
        for n, item in pairs:
            value = jnp.where(lane == n, item, value)
        target[...] = value

    def update_stage(batch, slot):
        del slot
        terms = [(n, step_terms(n, *spot(n))) for n in (5 * batch + k for k in range(5))]
        collect(norm1, [(n, t[0]) for n, t in terms])
        collect(dirsq, [(n, t[1]) for n, t in terms])

    def square_sum(column):
        square = column * column
        square = square[:16] + square[16:]
        return row_sum((square[:, :128] + square[:, 128:256]) + (square[:, 256:384] + square[:, 384:]))

    def norm_stage(batch, slot):
        del slot
        pairs = []
        for k in range(5):
            n = 5 * batch + k
            column = forward(second[n, 0].astype(BF16), second[n, 1].astype(BF16), smooth[n]) * 0.25
            pairs.append((n, square_sum(column)))
        collect(qsend.at[0], pairs)

    def update_phase(low, high):
        pipeline(
            low, high, lambda g: group_copy(i_pair, g).wait(), update_stage, norm_stage, lambda g: None
        )

    ends = (s_id == 0, s_id == n_sc - 1)
    gains = [jnp.where(end, 1.0 / 3.0, 0.25).astype(F32) for end in ends]
    halo_gains = [jnp.where(end, 0.0, 0.25).astype(F32) for end in ends]

    def edge_matched():
        for copy in halo_copies + other_copies:
            copy.wait()
        for c, side, n, f in edges:
            mine = adjoint(sample_rows(rx[c, f], 0), smooth[n])
            theirs = adjoint(sample_rows(rx_other[c, side], 1), halo[c, side])
            put(msend, n, [u * gains[side] + v * halo_gains[side] for u, v in zip(mine, theirs)], 1.0)
        edge_copy(m_pair).start()

    def edge_columns():
        edge_copy(m_pair).wait()
        for e, (c, side, n, f) in enumerate(edges):
            real, imag = [v.astype(BF16) for v in keep(total(msend, mrecv, n), c, f)]
            xsend[0, e] = (forward(real, imag, smooth[n]) * gains[side]).astype(BF16)
            xsend[1, e] = (forward(real, imag, halo[c, side]) * halo_gains[side]).astype(BF16)
        x_copy.start()

    def edge_image():
        x_copy.wait()
        for e, (c, side, n, f) in enumerate(edges):
            mine = (xsend[0, e].astype(F32) + xrecv[1, e].astype(F32)).astype(BF16)
            theirs = (xrecv[0, e].astype(F32) + xsend[1, e].astype(F32)).astype(BF16)
            mine, theirs = adjoint(mine, smooth[n]), adjoint(theirs, halo[c, side])
            put(isend, n, [u * gains[side] + v * halo_gains[side] for u, v in zip(mine, theirs)], 1.0)
        edge_copy(i_pair).start()

    def edge_update():
        edge_copy(i_pair).wait()
        terms = [(n, step_terms(n, c, f)) for c, side, n, f in edges]
        collect(norm1, [(n, t[0]) for n, t in terms])
        collect(dirsq, [(n, t[1]) for n, t in terms])
        for e, (c, side, n, f) in enumerate(edges):
            real, imag = second[n, 0].astype(BF16), second[n, 1].astype(BF16)
            ysend[e] = (forward(real, imag, halo[c, side]) * halo_gains[side]).astype(BF16)
            own2[e] = forward(real, imag, smooth[n]) * gains[side]
        y_copy.start()

    def edge_norm():
        y_copy.wait()
        collect(
            qsend.at[1],
            [(n, square_sum(own2[e] + yrecv[e].astype(F32))) for e, (c, side, n, f) in enumerate(edges)],
        )

    def q_copy(k):
        return remote(qsend.at[k], qrecv.at[k], q_ssem.at[k], q_rsem.at[k], partner)

    qsend[...] = jnp.zeros_like(qsend)
    norm1[...] = jnp.ones_like(norm1)
    dirsq[...] = jnp.ones_like(dirsq)

    image_phase(0, 4)
    edge_matched()
    image_phase(4, GROUPS)
    edge_columns()
    update_phase(0, 2)
    edge_image()
    update_phase(2, 4)
    edge_update()
    update_phase(4, GROUPS)
    q_copy(0).start()
    edge_norm()
    q_copy(1).start()

    def finish(n, c, f):
        alpha = row_sum(jnp.where(lane == n, alphas[n // (GROUPS * SIZE)], 0.0))
        for part in range(2):
            value = first[n, part] + alpha * second[n, part]
            for h in range(2):
                det[c, pl.ds((2 * part + h) * 256 + f * 8, 8), :] = value[8 * h : 8 * h + 8]

    def step_sizes(k):
        q_copy(k).wait()
        alphas[k] = norm1[...] / (qsend[k] + qrecv[k] + dirsq[...])

    def finish_phase(batch, _):
        for k in range(5):
            n = 5 * batch + k
            finish(n, *spot(n))
        return 0

    step_sizes(0)
    lax.fori_loop(0, 2 * GROUPS, finish_phase, 0)
    step_sizes(1)
    for c, side, n, f in edges:
        finish(n, c, f)

    def placed(which, c):
        a, s = which // SYM, which % SYM
        return det[c, pl.ds((2 * a + s // 8) * 256 + s % 8, BAND, stride=8), :].astype(BF16)

    for low in range(0, 2 * SYM, 8):
        high = min(low + 8, 2 * SYM)
        table = jnp.concatenate(
            [jnp.concatenate([placed(w, c) for w in range(low, high)], axis=0) for c in range(2)], axis=1
        )
        sent = lax.dot_general(
            onehot[...], table, (((1,), (1,)), ((), ())), preferred_element_type=F32
        )
        out[:, pl.ds(low * BAND, (high - low) * BAND)] = sent.astype(BF16)


def deliver_kernel(outgoing, arrived, ssem, rsem, lsem):
    c_id, p_id, s_id = lax.axis_index("cell"), lax.axis_index("panel"), lax.axis_index("sc")
    n_sc = lax.axis_size("sc")
    half = n_sc // 2
    barrier = pltpu.get_barrier_semaphore()
    origin = s_id // half

    def panel_to(other):
        return jnp.where(lax.rem(other, 2) == lax.rem(s_id, 2), p_id, 1 - p_id)

    def from_self(j):
        return (origin == c_id) & (j == s_id)

    def to_self(k):
        return (k // half == c_id) & (c_id * half + lax.rem(k, half) == s_id)

    def greet(j, _):
        @pl.when(jnp.logical_not(from_self(j)))
        def _():
            pl.semaphore_signal(barrier, inc=1, device_id=(origin, panel_to(j), j), device_id_type=MESH)

        return 0

    lax.fori_loop(0, n_sc, greet, 0)
    own = origin == c_id
    pl.semaphore_wait(barrier, n_sc - jnp.where(own, 1, 0))

    def target(i):
        k = lax.rem(i + s_id, n_sc)
        return k, c_id * half + lax.rem(k, half)

    def remote(k, other):
        return pltpu.make_async_remote_copy(
            src_ref=outgoing.at[k], dst_ref=arrived.at[s_id], send_sem=ssem.at[k], recv_sem=rsem.at[s_id],
            device_id=(k // half, panel_to(other), other), device_id_type=MESH,
        )

    def local(k):
        return pltpu.make_async_copy(outgoing.at[k], arrived.at[s_id], lsem)

    def send(i, _):
        k, other = target(i)

        @pl.when(to_self(k))
        def _():
            local(k).start()

        @pl.when(jnp.logical_not(to_self(k)))
        def _():
            remote(k, other).start()

        return 0

    lax.fori_loop(0, n_sc, send, 0)

    def finish(i, _):
        k, other = target(i)

        @pl.when(to_self(k))
        def _():
            local(k).wait()

        @pl.when(jnp.logical_not(to_self(k)))
        def _():
            remote(k, other).wait_send()

        @pl.when(jnp.logical_not(from_self(i)))
        def _():
            pltpu.make_async_remote_copy(
                src_ref=outgoing.at[0], dst_ref=arrived.at[i], send_sem=ssem.at[0], recv_sem=rsem.at[i],
                device_id=(origin, panel_to(i), i), device_id_type=MESH,
            ).wait_recv()

        return 0

    lax.fori_loop(0, n_sc, finish, 0)


ROWS = 2 * SYM * 16


def assemble_kernel(arrived, out, mixed, order):
    @pl.when(pl.program_id(0) == 0)
    def _():
        to = lax.broadcasted_iota(jnp.int32, (ROWS, ROWS), 0)
        source = lax.broadcasted_iota(jnp.int32, (ROWS, ROWS), 1)
        which, slot = source // 16, lax.rem(source, 16)
        goes = slot * (2 * SYM) + lax.rem(which, SYM) * 2 + which // SYM
        order[...] = jnp.where(to == goes, 1.0, 0.0).astype(BF16)

    lane = lax.broadcasted_iota(jnp.int32, (16, 128), 1)
    for half in range(2):
        for tile in range(7):
            blocks = [arrived[4 * half + k, :, pl.ds(128 * tile, 128)].astype(F32) for k in range(4)]
            for m in range(4):
                value = blocks[m]
                for k in range(4):
                    if k != m:
                        moved = pltpu.roll(blocks[k], (32 * (k - m)) % 128, 1)
                        inside = (lane >= 32 * k) & (lane < 32 * k + 32)
                        value = jnp.where(inside, moved, value)
                mixed[pl.ds((4 * tile + m) * 16, 16), pl.ds(128 * half, 128)] = value.astype(BF16)
    moved = jnp.dot(order[...], mixed[...], preferred_element_type=F32)
    for slot in range(16):
        rows = moved[slot * 2 * SYM : (slot + 1) * 2 * SYM]
        out[slot] = rows.astype(BF16).reshape(SYM, 2, 256)


def body(channel, received, noise_power, user_count, serving_cell):
    vmem = pltpu.VMEM
    keys = serving_cell.transpose(0, 2, 1)
    received = received.transpose(0, 1, 3, 2, 4)
    dma = pltpu.SemaphoreType.DMA
    outgoing = pl.pallas_call(
        detect_kernel,
        name="detect",
        out_shape=jax.ShapeDtypeStruct((512, 2 * SYM * BAND), BF16),
        in_specs=[
            pl.BlockSpec(memory_space=pl.ANY),
            pl.BlockSpec(memory_space=pl.ANY),
            pl.BlockSpec(memory_space=pltpu.SMEM),
            pl.BlockSpec(memory_space=pltpu.SMEM),
            pl.BlockSpec(memory_space=vmem),
        ],
        out_specs=pl.BlockSpec(memory_space=vmem),
        scratch_shapes=[
            vmem((2, BAND, 2, ANT, USERS), BF16),
            vmem((UNITS, ANT, 2 * USERS), BF16),
            vmem((2, BAND, 16, 2, ANT), BF16),
            vmem((2, 2, 16, 2, ANT), BF16),
            vmem((5, ANT // 128, 32, 128), F32),
            vmem((2, 2, ANT, 2 * USERS), BF16),
            vmem((UNITS, 2, SYM, USERS), BF16),
            vmem((UNITS, 2, SYM, USERS), BF16),
            vmem((UNITS, 2, SYM, USERS), BF16),
            vmem((UNITS, 2, SYM, USERS), BF16),
            vmem((2, 4, 32, ANT), BF16),
            vmem((2, 4, 32, ANT), BF16),
            vmem((4, 32, ANT), BF16),
            vmem((4, 32, ANT), BF16),
            vmem((4, 32, ANT), F32),
            vmem((2, 5, 32, ANT), BF16),
            vmem((2, 16, 128), F32),
            vmem((2, 16, 128), F32),
            vmem((2, 16, 128), F32),
            vmem((16, 128), F32),
            vmem((16, 128), F32),
            vmem((UNITS, 2, 16, USERS), F32),
            vmem((UNITS, 2, 16, USERS), F32),
            vmem((2, 1024, USERS), F32),
            vmem((512, 2 * USERS), BF16),
            dma((2, PER_CELL + 1)),
            dma((2,)),
            dma((2, 2, 2)),
            dma((2, 2, 2)),
            dma((2, 2)),
            dma((2, 2)),
            dma((GROUPS + 1,)),
            dma((GROUPS + 1,)),
            dma((GROUPS + 1,)),
            dma((GROUPS + 1,)),
            dma((2,)),
            dma((2,)),
            dma((2,)),
            dma((2,)),
        ],
        compiler_params=pltpu.CompilerParams(
            collective_id=0, has_side_effects=True, vmem_limit_bytes=60 * 1024 * 1024
        ),
    )(channel, received, noise_power, user_count, keys)
    arrived = pl.pallas_call(
        deliver_kernel,
        name="deliver",
        out_shape=jax.ShapeDtypeStruct((BAND, 16, 2 * SYM * BAND), BF16),
        in_specs=[pl.BlockSpec(memory_space=pl.ANY)],
        out_specs=pl.BlockSpec(memory_space=pl.ANY),
        scratch_shapes=[dma((32,)), dma((32,)), dma],
        compiler_params=pltpu.CompilerParams(collective_id=1, has_side_effects=True),
    )(outgoing.reshape(32, 16, 2 * SYM * BAND))
    routed = pl.pallas_call(
        assemble_kernel,
        name="assemble",
        grid=(4,),
        out_shape=jax.ShapeDtypeStruct((16, SYM, 2, 32 * BAND), BF16),
        in_specs=[pl.BlockSpec((8, 16, 2 * SYM * BAND), lambda i: (i, 0, 0))],
        out_specs=pl.BlockSpec((16, SYM, 2, 256), lambda i: (0, 0, 0, i)),
        scratch_shapes=[vmem((ROWS, 256), BF16), vmem((ROWS, ROWS), BF16)],
    )(arrived)
    return routed.reshape(2, 8, SYM, 2, 32 * BAND).transpose(0, 1, 3, 2, 4)


def solution(mesh):
    return jax.shard_map(
        body,
        mesh=mesh,
        in_specs=(
            P("cell", "sc", None, "panel", None),
            P("cell", "sc", None, None, "panel"),
            P("cell"),
            P("cell", "sc"),
            P("cell", None, None),
        ),
        out_specs=P("cell", "sc", None, None, None),
        check_vma=False,
    )
```

time: 103 us -> 83.6 us (0.81)
  Pallas kernels: 94.8 us -> 83.4 us
  local copies, waits for them, and re-layouts: 7.6 us -> 0 us
    pallas_call x1, Pallas kernels: 65.8 us -> 55.5 us  [body(): pl.pallas_call(detect_kernel, name='detect', out_shape=jax.ShapeDtypeStru...]
    reshape x2 -> x0, local copies, waits for them, and re-layouts: 3.9 us -> none  [the longest x1 3.1 us: body(): return routed.reshape(2, 8, 2, SYM, 32 * BAND)]
    unnamed x3 -> x0, local copies, waits for them, and re-layouts: 2 us -> none
    pallas_call x1, Pallas kernels: 6.25 us -> 4.45 us  [body(): pl.pallas_call(assemble_kernel, name='assemble', grid=(4,), out_shape=jax...]
    pad x1 -> x0, local copies, waits for them, and re-layouts: 1.71 us -> none  [body(): received = jnp.pad(received, ((0, 0), (0, 0), (0, 0), (0, 2), (0, 0)))]
where the time goes in v2:
time: 83.6 us; the launch traced here: 83.4 us
  Pallas kernels  83.4 us (100%)
    pallas_call x1, Pallas kernels, body(): pl.pallas_call(detect_kernel, name='detect', out_shape=jax.ShapeDtypeStru...  55.5 us
    pallas_call x1, Pallas kernels, body(): pl.pallas_call(deliver_kernel, name='deliver', out_shape=jax.ShapeDtypeSt...  23.5 us
    pallas_call x1, Pallas kernels, body(): pl.pallas_call(assemble_kernel, name='assemble', grid=(4,), out_shape=jax...  4.45 us

profile of v2, /device:TPU:1, one launch (start us, length us, event | category | flops | bytes accessed | tf_op | source)
XLA Modules:
  0.0 83.4 jit_solution(8303485799766250325)
XLA Ops:
  0.0 55.5 %detect.1 = bf16[512,896]{1,0:T(8,128)(2,1)} custom-call(bf16[2,32,2,512,128]{4,3,2,1,0:T(8,128)(2,1)} %channel.1, bf16[2,32,14,2,512]{4,3,2,1,0:T(2,128)(2,1)} %bitcast.7, f32[2]{0:T(128)} %noise.1, s32[2,2]{1,0:T(2,128)} %counts.1, s32[2,1,128]{2,1,0:T(1,128)} %bitcast.8), custom_call_target="tpu_custom_call" | custom-call | tf_op jit(solution)/shard_map/detect/pallas_call | solution.py:509
  55.5 23.5 %deliver.1.arrived = bf16[32,16,896]{2,1,0:T(8,128)(2,1)} custom-call(bf16[32,16,896]{2,1,0:T(8,128)(2,1)} %bitcast.6), custom_call_target="tpu_custom_call" | custom-call | tf_op jit(solution)/shard_map/deliver/pallas_call | solution.py:566
  79.0 4.4 %assemble.1 = bf16[16,14,2,1024]{3,2,1,0:T(2,128)(2,1)} custom-call(bf16[32,16,896]{2,1,0:T(8,128)(2,1)} %deliver.1.arrived), custom_call_target="tpu_custom_call" | custom-call | tf_op jit(solution)/shard_map/assemble/pallas_call | solution.py:575

commit v3 on v2

v3 whole, which is shorter than its diff:
```python
import functools

import jax
import jax.numpy as jnp
from jax import lax
from jax.experimental import pallas as pl
from jax.experimental.pallas import tpu as pltpu
from jax.sharding import PartitionSpec as P

GRP = 16
MESH = pl.DeviceIdType.MESH
F32, BF16 = jnp.float32, jnp.bfloat16

BAND, ANT, USERS, SYM = 32, 512, 128, 14
INNER = BAND - 2
SIZE = 10
PER_CELL = INNER // SIZE
GROUPS = 2 * PER_CELL
UNITS = 2 * BAND


def combine(out):
    return out[:16, :128] + out[16:, 128:], out[16:, :128] - out[:16, 128:]


def adjoint(rows, block):
    return combine(jnp.dot(rows, block, preferred_element_type=F32))


def forward(real, imag, block):
    left = jnp.concatenate(
        [jnp.concatenate([real, -imag], axis=1), jnp.concatenate([imag, real], axis=1)], axis=0
    )
    return lax.dot_general(left, block, (((1,), (1,)), ((), ())), preferred_element_type=F32)


def row_sum(values):
    return jnp.sum(values, axis=1, keepdims=True)


def detect_kernel(
    channel, received, noise, counts, keys, arrived,
    raw, smooth, gram, edge, rx, rx_other, split, halo, msend, mrecv, isend, irecv, xsend, xrecv, ysend, yrecv,
    qsend, qrecv, alphas, norm1, dirsq, first, second, det, onehot, outgoing,
    raw_sem, rx_sem, halo_ssem, halo_rsem, o_ssem, o_rsem, m_ssem, m_rsem, i_ssem, i_rsem,
    x_ssem, x_rsem, q_ssem, q_rsem, d_ssem, d_rsem, d_lsem,
):
    c_id, p_id, s_id = lax.axis_index("cell"), lax.axis_index("panel"), lax.axis_index("sc")
    n_sc = lax.axis_size("sc")
    partner = (c_id, 1 - p_id, s_id)
    upper = (c_id, 1 - p_id, lax.rem(s_id + 1, n_sc))
    lower = (c_id, 1 - p_id, lax.rem(s_id + n_sc - 1, n_sc))
    edges = [(c, side, GROUPS * SIZE + 2 * c + side, side * (BAND - 1)) for c in range(2) for side in range(2)]

    def raw_copy(c, k):
        rows = pl.ds(k * SIZE + 2, SIZE)
        return pltpu.make_async_copy(channel.at[c, rows], raw.at[c, rows], raw_sem.at[c, k])

    def head_copy(c):
        rows = pl.ds(0, 2)
        return pltpu.make_async_copy(channel.at[c, rows], raw.at[c, rows], raw_sem.at[c, PER_CELL])

    def rx_copy(c):
        return pltpu.make_async_copy(received.at[c], rx.at[c, :, pl.ds(0, SYM)], rx_sem.at[c])

    for c in range(2):
        head_copy(c).start()
        rx_copy(c).start()
        for k in range(PER_CELL):
            raw_copy(c, k).start()

    barrier = pltpu.get_barrier_semaphore()
    for device in (partner, upper, lower):
        pl.semaphore_signal(barrier, inc=1, device_id=device, device_id_type=MESH)

    half = n_sc // 2
    origin = s_id // half

    def panel_to(other):
        return jnp.where(lax.rem(other, 2) == lax.rem(s_id, 2), p_id, 1 - p_id)

    def from_self(j):
        return (origin == c_id) & (j == s_id)

    def greet(j, _):
        @pl.when(jnp.logical_not(from_self(j)))
        def _():
            pl.semaphore_signal(barrier, inc=1, device_id=(origin, panel_to(j), j), device_id_type=MESH)

        return 0

    lax.fori_loop(0, n_sc, greet, 0)
    pl.semaphore_wait(barrier, 3 + n_sc - jnp.where(origin == c_id, 1, 0))

    def remote(source, target, ssem, rsem, device):
        return pltpu.make_async_remote_copy(
            src_ref=source, dst_ref=target, send_sem=ssem, recv_sem=rsem,
            device_id=device, device_id_type=MESH,
        )

    other_copies = [
        remote(
            received.at[c, f], rx_other.at[c, side, pl.ds(0, SYM)],
            o_ssem.at[c, side], o_rsem.at[c, side], partner,
        )
        for c, side, n, f in edges
    ]
    halo_copies = [
        remote(
            channel.at[c, BAND - 1 - f, part], halo.at[c, side, :, pl.ds(128 * part, 128)],
            halo_ssem.at[c, side, part], halo_rsem.at[c, side, part], (upper, lower)[side],
        )
        for c, side, n, f in edges
        for part in range(2)
    ]
    for copy in halo_copies + other_copies:
        copy.start()

    def group_copy(pair, g):
        source, target, ssem, rsem = pair
        rows = pl.ds(g * SIZE, SIZE)
        return remote(source.at[rows], target.at[rows], ssem.at[g], rsem.at[g], partner)

    def edge_copy(pair, c):
        source, target, ssem, rsem = pair
        rows = pl.ds(GROUPS * SIZE + 2 * c, 2)
        return remote(source.at[rows], target.at[rows], ssem.at[GROUPS + c], rsem.at[GROUPS + c], partner)

    m_pair = (msend, mrecv, m_ssem, m_rsem)
    i_pair = (isend, irecv, i_ssem, i_rsem)

    def x_copy(c):
        return remote(xsend.at[c], xrecv.at[c], x_ssem.at[0, c], x_rsem.at[0, c], partner)

    def y_copy(c):
        return remote(ysend.at[c], yrecv.at[c], x_ssem.at[1, c], x_rsem.at[1, c], partner)

    lane = lax.broadcasted_iota(jnp.int32, (16, 128), 1)

    users2 = 2 * USERS
    key_row = jnp.concatenate([keys[0], keys[1]], axis=1).astype(F32)
    rows_i = lax.broadcasted_iota(jnp.int32, (users2, users2), 0)
    cols_i = lax.broadcasted_iota(jnp.int32, (users2, users2), 1)
    key_f = jnp.sum(jnp.where(rows_i == cols_i, key_row, 0.0), axis=1, keepdims=True)
    earlier = (key_f == key_row) & (rows_i < cols_i)
    rank_row = jnp.sum(jnp.where(earlier, 1.0, 0.0), axis=0, keepdims=True).astype(jnp.int32)
    key_row = key_row.astype(jnp.int32)
    place = (key_row // 2) * 256 + (rank_row // 8) * 16 + lax.rem(key_row, 2) * 8 + lax.rem(rank_row, 8)
    for row in range(0, 512, 64):
        slot = lax.broadcasted_iota(jnp.int32, (64, users2), 0) + row
        onehot[pl.ds(row, 64), :] = jnp.where(slot == place, 1.0, 0.0).astype(BF16)

    def spot(n):
        c = n // INNER
        return c, lax.rem(n, INNER) + 1

    def keep(values, c, f):
        mask = lane < counts[c, f // GRP]
        return [jnp.where(mask, v, 0.0) for v in values]

    def total(mine, theirs, n):
        pad = jnp.zeros((2, USERS), F32)
        return [
            jnp.concatenate([mine[n, a].astype(F32) + theirs[n, a].astype(F32), pad], axis=0)
            for a in range(2)
        ]

    def put(target, n, values, gain):
        for a in range(2):
            target[n, a] = (values[a][:SYM] * gain).astype(BF16)

    def sample_rows(block, k):
        both = block.reshape(32, ANT).astype(F32)
        for tile in range(ANT // 128):
            split[k, tile] = both[:, 128 * tile : 128 * tile + 128]
        return jnp.concatenate(
            [
                jnp.concatenate(
                    [split.at[k, tile][pl.ds(a, 16, stride=2), :] for tile in range(ANT // 128)], axis=1
                )
                for a in range(2)
            ],
            axis=0,
        ).astype(BF16)

    for c in range(2):
        head_copy(c).wait()
        rx_copy(c).wait()

    def smooth_stage(batch, slot):
        c, base = batch // (2 * PER_CELL), lax.rem(batch, 2 * PER_CELL) * 5
        for part in range(2):
            for row in range(0, ANT, 32):
                rows = pl.ds(row, 32)
                low, here = raw[c, base, part, rows, :], raw[c, base + 1, part, rows, :]
                for k in range(5):
                    high = raw[c, base + k + 2, part, rows, :]
                    smooth[slot, k, rows, pl.ds(128 * part, 128)] = (low + high) + (here + here)
                    low, here = here, high

    def gram_stage(batch, slot):
        for k in range(5):
            n = 5 * batch + k
            c, f = spot(n)
            block = smooth[slot, k]
            left = jnp.concatenate([block.T, sample_rows(rx[c, f], k)], axis=0)
            product = jnp.dot(left, block, preferred_element_type=F32)
            gram[n, pl.ds(0, 128), :] = (product[:128, :128] + product[128:256, 128:]).astype(BF16)
            gram[n, pl.ds(128, 128), :] = (product[:128, 128:] - product[128:256, :128]).astype(BF16)
            put(msend, n, combine(product[256:]), 0.25)

    def gram_apply(n, real, imag):
        real, imag = real.astype(BF16), imag.astype(BF16)
        left = jnp.concatenate(
            [jnp.concatenate([real, imag], axis=1), jnp.concatenate([imag, -real], axis=1)], axis=0
        )
        result = jnp.dot(left, gram[n], preferred_element_type=F32)
        return result[:16], result[16:]

    def image_phase(g):
        group_copy(m_pair, g).wait()

        def step(i, _):
            for k in range(5):
                n = g * SIZE + 5 * i + k
                put(isend, n, gram_apply(n, *keep(total(msend, mrecv, n), *spot(n))), 0.0625)
            return 0

        lax.fori_loop(0, SIZE // 5, step, 0)
        group_copy(i_pair, g).start()

    def step_terms(n, c, f):
        power = noise[c]
        br, bi = keep(total(msend, mrecv, n), c, f)
        ir, ii = keep(total(isend, irecv, n), c, f)
        ir, ii = ir + power * br, ii + power * bi
        norm0 = row_sum(br * br + bi * bi)
        alpha = norm0 / row_sum(br * ir + bi * ii)
        first[n, 0], first[n, 1] = alpha * br, alpha * bi
        rr, ri = br - alpha * ir, bi - alpha * ii
        norm = row_sum(rr * rr + ri * ri)
        beta = norm / norm0
        dr, di = rr + beta * br, ri + beta * bi
        second[n, 0], second[n, 1] = dr, di
        return norm, power * row_sum(dr * dr + di * di), dr, di

    def collect(target, pairs):
        value = target[...]
        for n, item in pairs:
            value = jnp.where(lane == n, item, value)
        target[...] = value

    def update_phase(g):
        group_copy(i_pair, g).wait()

        def step(i, _):
            spots = [g * SIZE + 5 * i + k for k in range(5)]
            terms = [step_terms(n, *spot(n)) for n in spots]
            squares = []
            for n, (_norm, _dirsq, dr, di) in zip(spots, terms):
                gr, gi = gram_apply(n, dr, di)
                squares.append(row_sum(dr * gr + di * gi) * 0.0625)
            collect(norm1, [(n, t[0]) for n, t in zip(spots, terms)])
            collect(dirsq, [(n, t[1]) for n, t in zip(spots, terms)])
            collect(qsend.at[0], list(zip(spots, squares)))
            return 0

        lax.fori_loop(0, SIZE // 5, step, 0)

    def square_sum(column):
        square = column * column
        square = square[:16] + square[16:]
        return row_sum((square[:, :128] + square[:, 128:256]) + (square[:, 256:384] + square[:, 384:]))

    ends = (s_id == 0, s_id == n_sc - 1)
    gains = [jnp.where(end, 1.0 / 3.0, 0.25).astype(F32) for end in ends]
    halo_gains = [jnp.where(end, 0.0, 0.25).astype(F32) for end in ends]

    def own_edges(cell):
        return [(2 * cell + side, side, GROUPS * SIZE + 2 * cell + side, side * (BAND - 1)) for side in range(2)]

    def edge_matched(c):
        for copy in halo_copies[4 * c : 4 * c + 4] + other_copies[2 * c : 2 * c + 2]:
            copy.wait()
        for e, side, n, f in own_edges(c):
            mine = adjoint(sample_rows(rx[c, f], 0), edge[e])
            theirs = adjoint(sample_rows(rx_other[c, side], 1), halo[c, side])
            put(msend, n, [u * gains[side] + v * halo_gains[side] for u, v in zip(mine, theirs)], 1.0)
        edge_copy(m_pair, c).start()

    def edge_products(target, c, real, imag, e, side):
        target[c, 0, side] = (forward(real, imag, edge[e]) * gains[side]).astype(BF16)
        target[c, 1, side] = (forward(real, imag, halo[c, side]) * halo_gains[side]).astype(BF16)

    def edge_sums(sent, got, c, side):
        mine = sent[c, 0, side].astype(F32) + got[c, 1, side].astype(F32)
        theirs = got[c, 0, side].astype(F32) + sent[c, 1, side].astype(F32)
        return mine, theirs

    def edge_columns(c):
        edge_copy(m_pair, c).wait()
        for e, side, n, f in own_edges(c):
            real, imag = [v.astype(BF16) for v in keep(total(msend, mrecv, n), c, f)]
            edge_products(xsend, c, real, imag, e, side)
        x_copy(c).start()

    def edge_image(c):
        x_copy(c).wait()
        for e, side, n, f in own_edges(c):
            mine, theirs = [v.astype(BF16) for v in edge_sums(xsend, xrecv, c, side)]
            mine, theirs = adjoint(mine, edge[e]), adjoint(theirs, halo[c, side])
            put(isend, n, [u * gains[side] + v * halo_gains[side] for u, v in zip(mine, theirs)], 1.0)
        edge_copy(i_pair, c).start()

    def edge_update(c):
        edge_copy(i_pair, c).wait()
        found = own_edges(c)
        terms = [(n, step_terms(n, c, f)) for e, side, n, f in found]
        collect(norm1, [(n, t[0]) for n, t in terms])
        collect(dirsq, [(n, t[1]) for n, t in terms])
        for (e, side, n, f), (_n, t) in zip(found, terms):
            edge_products(ysend, c, t[2].astype(BF16), t[3].astype(BF16), e, side)
        y_copy(c).start()

    def edge_norm(c):
        y_copy(c).wait()
        pairs = []
        for e, side, n, f in own_edges(c):
            mine, theirs = edge_sums(ysend, yrecv, c, side)
            pairs.append((n, square_sum(mine) + square_sum(theirs)))
        collect(qsend.at[1], pairs)

    q_copy = remote(qsend.at[0], qrecv, q_ssem, q_rsem, partner)

    qsend[...] = jnp.zeros_like(qsend)
    norm1[...] = jnp.ones_like(norm1)
    dirsq[...] = jnp.ones_like(dirsq)

    def finish(n, c, f):
        alpha = row_sum(jnp.where(lane == n, alphas[n // (GROUPS * SIZE)], 0.0))
        for part in range(2):
            value = first[n, part] + alpha * second[n, part]
            for h in range(2):
                det[c, pl.ds((2 * part + h) * 256 + f * 8, 8), :] = value[8 * h : 8 * h + 8]

    def step_sizes(k):
        if k == 0:
            q_copy.wait()
        square = qsend[0] + qrecv[...] if k == 0 else qsend[1]
        alphas[k] = norm1[...] / (square + dirsq[...])

    def finish_phase(batch, _):
        for k in range(5):
            n = 5 * batch + k
            finish(n, *spot(n))
        return 0

    def edge_blocks(c):
        def strip(i, _):
            rows = pl.ds(pl.multiple_of(i * 64, 64), 64)
            for e, side, n, f in own_edges(c):
                for part in range(2):
                    here, inner = raw[c, f, part, rows, :], raw[c, 1 + side * (BAND - 3), part, rows, :]
                    edge[e, rows, pl.ds(128 * part, 128)] = inner + (here + here)
            return 0

        lax.fori_loop(0, ANT // 64, strip, 0)

    def raw_wait(g):
        raw_copy(g // PER_CELL, lax.rem(g, PER_CELL)).wait()

    raw_wait(0)
    smooth_stage(0, 0)

    def main_step(g, _):
        gram_stage(2 * g, 0)
        smooth_stage(2 * g + 1, 1)
        raw_wait(g + 1)
        gram_stage(2 * g + 1, 1)
        smooth_stage(2 * g + 2, 0)
        group_copy(m_pair, g).start()

        @pl.when(g >= 1)
        def _():
            image_phase(g - 1)

        @pl.when(g >= 2)
        def _():
            update_phase(g - 2)

        @pl.when(g == 2)
        def _():
            edge_blocks(0)
            edge_matched(0)

        @pl.when(g == 3)
        def _():
            edge_columns(0)

        @pl.when(g == 4)
        def _():
            edge_blocks(1)
            edge_matched(1)
            edge_image(0)

        return 0

    last = GROUPS - 1
    lax.fori_loop(0, last, main_step, 0)
    gram_stage(2 * last, 0)
    smooth_stage(2 * last + 1, 1)
    edge_columns(1)
    gram_stage(2 * last + 1, 1)
    group_copy(m_pair, last).start()
    image_phase(last - 1)
    edge_update(0)
    update_phase(last - 2)
    edge_image(1)
    image_phase(last)
    update_phase(last - 1)
    edge_update(1)
    update_phase(last)
    q_copy.start()
    edge_norm(0)
    edge_norm(1)
    step_sizes(1)
    for c, side, n, f in edges:
        finish(n, c, f)
    step_sizes(0)
    lax.fori_loop(0, 2 * GROUPS, finish_phase, 0)

    def placed(which, c):
        a, s = which // SYM, which % SYM
        return det[c, pl.ds((2 * a + s // 8) * 256 + s % 8, BAND, stride=8), :].astype(BF16)

    for low in range(0, 2 * SYM, 8):
        high = min(low + 8, 2 * SYM)
        table = jnp.concatenate(
            [jnp.concatenate([placed(w, c) for w in range(low, high)], axis=0) for c in range(2)], axis=1
        )
        sent = lax.dot_general(
            onehot[...], table, (((1,), (1,)), ((), ())), preferred_element_type=F32
        )
        sent = sent.astype(BF16).reshape(32, 16, (high - low) * BAND)
        outgoing[:, :, pl.ds(low * BAND, (high - low) * BAND)] = sent

    def target(i):
        k = lax.rem(i + s_id, n_sc)
        return k, c_id * half + lax.rem(k, half)

    def to_self(k):
        return (k // half == c_id) & (c_id * half + lax.rem(k, half) == s_id)

    def parcel(k, other):
        return remote(
            outgoing.at[k], arrived.at[s_id], d_ssem.at[k], d_rsem.at[s_id], (k // half, panel_to(other), other)
        )

    def local_parcel(k):
        return pltpu.make_async_copy(outgoing.at[k], arrived.at[s_id], d_lsem)

    def send(i, _):
        k, other = target(i)

        @pl.when(to_self(k))
        def _():
            local_parcel(k).start()

        @pl.when(jnp.logical_not(to_self(k)))
        def _():
            parcel(k, other).start()

        return 0

    lax.fori_loop(0, n_sc, send, 0)

    def settle(i, _):
        k, other = target(i)

        @pl.when(to_self(k))
        def _():
            local_parcel(k).wait()

        @pl.when(jnp.logical_not(to_self(k)))
        def _():
            parcel(k, other).wait_send()

        @pl.when(jnp.logical_not(from_self(i)))
        def _():
            remote(
                outgoing.at[0], arrived.at[i], d_ssem.at[0], d_rsem.at[i], (origin, panel_to(i), i)
            ).wait_recv()

        return 0

    lax.fori_loop(0, n_sc, settle, 0)


ROWS = 2 * SYM * 16


def assemble_kernel(arrived, out, mixed, order):
    @pl.when(pl.program_id(0) == 0)
    def _():
        to = lax.broadcasted_iota(jnp.int32, (ROWS, ROWS), 0)
        source = lax.broadcasted_iota(jnp.int32, (ROWS, ROWS), 1)
        which, slot = source // 16, lax.rem(source, 16)
        goes = slot * (2 * SYM) + lax.rem(which, SYM) * 2 + which // SYM
        order[...] = jnp.where(to == goes, 1.0, 0.0).astype(BF16)

    lane = lax.broadcasted_iota(jnp.int32, (16, 128), 1)
    for half in range(2):
        for tile in range(7):
            blocks = [arrived[4 * half + k, :, pl.ds(128 * tile, 128)].astype(F32) for k in range(4)]
            for m in range(4):
                value = blocks[m]
                for k in range(4):
                    if k != m:
                        moved = pltpu.roll(blocks[k], (32 * (k - m)) % 128, 1)
                        inside = (lane >= 32 * k) & (lane < 32 * k + 32)
                        value = jnp.where(inside, moved, value)
                mixed[pl.ds((4 * tile + m) * 16, 16), pl.ds(128 * half, 128)] = value.astype(BF16)
    moved = jnp.dot(order[...], mixed[...], preferred_element_type=F32)
    for slot in range(16):
        rows = moved[slot * 2 * SYM : (slot + 1) * 2 * SYM]
        out[slot] = rows.astype(BF16).reshape(SYM, 2, 256)


def body(channel, received, noise_power, user_count, serving_cell):
    vmem = pltpu.VMEM
    keys = serving_cell.transpose(0, 2, 1)
    received = received.transpose(0, 1, 3, 2, 4)
    dma = pltpu.SemaphoreType.DMA
    arrived = pl.pallas_call(
        detect_kernel,
        name="detect",
        out_shape=jax.ShapeDtypeStruct((32, 16, 2 * SYM * BAND), BF16),
        in_specs=[
            pl.BlockSpec(memory_space=pl.ANY),
            pl.BlockSpec(memory_space=pl.ANY),
            pl.BlockSpec(memory_space=pltpu.SMEM),
            pl.BlockSpec(memory_space=pltpu.SMEM),
            pl.BlockSpec(memory_space=vmem),
        ],
        out_specs=pl.BlockSpec(memory_space=pl.ANY),
        scratch_shapes=[
            vmem((2, BAND, 2, ANT, USERS), BF16),
            vmem((2, 5, ANT, 2 * USERS), BF16),
            vmem((GROUPS * SIZE, 2 * USERS, USERS), BF16),
            vmem((4, ANT, 2 * USERS), BF16),
            vmem((2, BAND, 16, 2, ANT), BF16),
            vmem((2, 2, 16, 2, ANT), BF16),
            vmem((5, ANT // 128, 32, 128), F32),
            vmem((2, 2, ANT, 2 * USERS), BF16),
            vmem((UNITS, 2, SYM, USERS), BF16),
            vmem((UNITS, 2, SYM, USERS), BF16),
            vmem((UNITS, 2, SYM, USERS), BF16),
            vmem((UNITS, 2, SYM, USERS), BF16),
            vmem((2, 2, 2, 32, ANT), BF16),
            vmem((2, 2, 2, 32, ANT), BF16),
            vmem((2, 2, 2, 32, ANT), BF16),
            vmem((2, 2, 2, 32, ANT), BF16),
            vmem((2, 16, 128), F32),
            vmem((16, 128), F32),
            vmem((2, 16, 128), F32),
            vmem((16, 128), F32),
            vmem((16, 128), F32),
            vmem((UNITS, 2, 16, USERS), F32),
            vmem((UNITS, 2, 16, USERS), F32),
            vmem((2, 1024, USERS), F32),
            vmem((512, 2 * USERS), BF16),
            vmem((32, 16, 2 * SYM * BAND), BF16),
            dma((2, PER_CELL + 1)),
            dma((2,)),
            dma((2, 2, 2)),
            dma((2, 2, 2)),
            dma((2, 2)),
            dma((2, 2)),
            dma((GROUPS + 2,)),
            dma((GROUPS + 2,)),
            dma((GROUPS + 2,)),
            dma((GROUPS + 2,)),
            dma((2, 2)),
            dma((2, 2)),
            dma,
            dma,
            dma((32,)),
            dma((32,)),
            dma,
        ],
        compiler_params=pltpu.CompilerParams(
            collective_id=0, has_side_effects=True, vmem_limit_bytes=60 * 1024 * 1024
        ),
    )(channel, received, noise_power, user_count, keys)
    routed = pl.pallas_call(
        assemble_kernel,
        name="assemble",
        grid=(4,),
        out_shape=jax.ShapeDtypeStruct((16, SYM, 2, 32 * BAND), BF16),
        in_specs=[pl.BlockSpec((8, 16, 2 * SYM * BAND), lambda i: (i, 0, 0))],
        out_specs=pl.BlockSpec((16, SYM, 2, 256), lambda i: (0, 0, 0, i)),
        scratch_shapes=[vmem((ROWS, 256), BF16), vmem((ROWS, ROWS), BF16)],
    )(arrived)
    return routed.reshape(2, 8, SYM, 2, 32 * BAND).transpose(0, 1, 3, 2, 4)


def solution(mesh):
    return jax.shard_map(
        body,
        mesh=mesh,
        in_specs=(
            P("cell", "sc", None, "panel", None),
            P("cell", "sc", None, None, "panel"),
            P("cell"),
            P("cell", "sc"),
            P("cell", None, None),
        ),
        out_specs=P("cell", "sc", None, None, None),
        check_vma=False,
    )
```

time: 83.6 us -> 76.4 us (0.914)
  Pallas kernels: 83.4 us -> 76.3 us
    pallas_call x1 -> x0, Pallas kernels: 23.5 us -> none  [body(): pl.pallas_call(deliver_kernel, name='deliver', out_shape=jax.ShapeDtypeSt...]
    pallas_call x1, Pallas kernels: 55.5 us -> 71.8 us  [body(): pl.pallas_call(detect_kernel, name='detect', out_shape=jax.ShapeDtypeStru...]
where the time goes in v3:
time: 76.4 us; the launch traced here: 76.3 us
  Pallas kernels  76.3 us (100%)
    pallas_call x1, Pallas kernels, body(): pl.pallas_call(detect_kernel, name='detect', out_shape=jax.ShapeDtypeStru...  71.8 us
    pallas_call x1, Pallas kernels, body(): pl.pallas_call(assemble_kernel, name='assemble', grid=(4,), out_shape=jax...  4.45 us

profile of v3, /device:TPU:1, one launch (start us, length us, event | category | flops | bytes accessed | tf_op | source)
XLA Modules:
  0.0 76.3 jit_solution(6876327920535866504)
XLA Ops:
  0.0 71.8 %detect.1.arrived = bf16[32,16,896]{2,1,0:T(8,128)(2,1)} custom-call(bf16[2,32,2,512,128]{4,3,2,1,0:T(8,128)(2,1)} %channel.1, bf16[2,32,14,2,512]{4,3,2,1,0:T(2,128)(2,1)} %bitcast.5, f32[2]{0:T(128)} %noise.1, s32[2,2]{1,0:T(2,128)} %counts.1, s32[2,1,128]{2,1,0:T(1,128)} %bitcast.6), custom_call_target="tpu_custom_call" | custom-call | tf_op jit(solution)/shard_map/detect/pallas_call | solution.py:534
  71.8 4.4 %assemble.1 = bf16[16,14,2,1024]{3,2,1,0:T(2,128)(2,1)} custom-call(bf16[32,16,896]{2,1,0:T(8,128)(2,1)} %detect.1.arrived), custom_call_target="tpu_custom_call" | custom-call | tf_op jit(solution)/shard_map/assemble/pallas_call | solution.py:595

commit v4 on v3

--- a/solution.py
+++ b/solution.py
@@ -40,7 +40,7 @@
 
 def detect_kernel(
     channel, received, noise, counts, keys, arrived,
-    raw, smooth, gram, edge, rx, rx_other, split, halo, msend, mrecv, isend, irecv, xsend, xrecv, ysend, yrecv,
+    raw, smooth, gram, edge, rx, rx_other, split, halo, msend, mrecv, isend, irecv, xsend, xrecv, ysend, yrecv, own2,
     qsend, qrecv, alphas, norm1, dirsq, first, second, det, onehot, outgoing,
     raw_sem, rx_sem, halo_ssem, halo_rsem, o_ssem, o_rsem, m_ssem, m_rsem, i_ssem, i_rsem,
     x_ssem, x_rsem, q_ssem, q_rsem, d_ssem, d_rsem, d_lsem,
@@ -288,13 +288,21 @@
             put(msend, n, [u * gains[side] + v * halo_gains[side] for u, v in zip(mine, theirs)], 1.0)
         edge_copy(m_pair, c).start()
 
+    def pack(target, column):
+        for a in range(2):
+            target[a] = column[16 * a : 16 * a + SYM].astype(BF16)
+
+    def unpack(source):
+        pad = jnp.zeros((2, ANT), F32)
+        return jnp.concatenate([source[0].astype(F32), pad, source[1].astype(F32), pad], axis=0)
+
     def edge_products(target, c, real, imag, e, side):
-        target[c, 0, side] = (forward(real, imag, edge[e]) * gains[side]).astype(BF16)
-        target[c, 1, side] = (forward(real, imag, halo[c, side]) * halo_gains[side]).astype(BF16)
+        pack(target.at[c, 0, side], forward(real, imag, edge[e]) * gains[side])
+        pack(target.at[c, 1, side], forward(real, imag, halo[c, side]) * halo_gains[side])
 
     def edge_sums(sent, got, c, side):
-        mine = sent[c, 0, side].astype(F32) + got[c, 1, side].astype(F32)
-        theirs = got[c, 0, side].astype(F32) + sent[c, 1, side].astype(F32)
+        mine = unpack(sent.at[c, 0, side]) + unpack(got.at[c, 1, side])
+        theirs = unpack(got.at[c, 0, side]) + unpack(sent.at[c, 1, side])
         return mine, theirs
 
     def edge_columns(c):
@@ -319,18 +327,20 @@
         collect(norm1, [(n, t[0]) for n, t in terms])
         collect(dirsq, [(n, t[1]) for n, t in terms])
         for (e, side, n, f), (_n, t) in zip(found, terms):
-            edge_products(ysend, c, t[2].astype(BF16), t[3].astype(BF16), e, side)
+            real, imag = t[2].astype(BF16), t[3].astype(BF16)
+            pack(ysend.at[c, side], forward(real, imag, halo[c, side]) * halo_gains[side])
+            own2[e] = forward(real, imag, edge[e]) * gains[side]
         y_copy(c).start()
 
     def edge_norm(c):
         y_copy(c).wait()
-        pairs = []
-        for e, side, n, f in own_edges(c):
-            mine, theirs = edge_sums(ysend, yrecv, c, side)
-            pairs.append((n, square_sum(mine) + square_sum(theirs)))
-        collect(qsend.at[1], pairs)
-
-    q_copy = remote(qsend.at[0], qrecv, q_ssem, q_rsem, partner)
+        collect(
+            qsend.at[1],
+            [(n, square_sum(own2[e] + unpack(yrecv.at[c, side]))) for e, side, n, f in own_edges(c)],
+        )
+
+    def q_copy(k):
+        return remote(qsend.at[k], qrecv.at[k], q_ssem.at[k], q_rsem.at[k], partner)
 
     qsend[...] = jnp.zeros_like(qsend)
     norm1[...] = jnp.ones_like(norm1)
@@ -344,10 +354,8 @@
                 det[c, pl.ds((2 * part + h) * 256 + f * 8, 8), :] = value[8 * h : 8 * h + 8]
 
     def step_sizes(k):
-        if k == 0:
-            q_copy.wait()
-        square = qsend[0] + qrecv[...] if k == 0 else qsend[1]
-        alphas[k] = norm1[...] / (square + dirsq[...])
+        q_copy(k).wait()
+        alphas[k] = norm1[...] / (qsend[k] + qrecv[k] + dirsq[...])
 
     def finish_phase(batch, _):
         for k in range(5):
@@ -420,14 +428,15 @@
     update_phase(last - 1)
     edge_update(1)
     update_phase(last)
-    q_copy.start()
+    q_copy(0).start()
     edge_norm(0)
     edge_norm(1)
+    q_copy(1).start()
+    step_sizes(0)
+    lax.fori_loop(0, 2 * GROUPS, finish_phase, 0)
     step_sizes(1)
     for c, side, n, f in edges:
         finish(n, c, f)
-    step_sizes(0)
-    lax.fori_loop(0, 2 * GROUPS, finish_phase, 0)
 
     def placed(which, c):
         a, s = which // SYM, which % SYM
@@ -556,12 +565,13 @@
             vmem((UNITS, 2, SYM, USERS), BF16),
             vmem((UNITS, 2, SYM, USERS), BF16),
             vmem((UNITS, 2, SYM, USERS), BF16),
-            vmem((2, 2, 2, 32, ANT), BF16),
-            vmem((2, 2, 2, 32, ANT), BF16),
-            vmem((2, 2, 2, 32, ANT), BF16),
-            vmem((2, 2, 2, 32, ANT), BF16),
+            vmem((2, 2, 2, 2, SYM, ANT), BF16),
+            vmem((2, 2, 2, 2, SYM, ANT), BF16),
+            vmem((2, 2, 2, SYM, ANT), BF16),
+            vmem((2, 2, 2, SYM, ANT), BF16),
+            vmem((4, 32, ANT), F32),
             vmem((2, 16, 128), F32),
-            vmem((16, 128), F32),
+            vmem((2, 16, 128), F32),
             vmem((2, 16, 128), F32),
             vmem((16, 128), F32),
             vmem((16, 128), F32),
@@ -582,8 +592,8 @@
             dma((GROUPS + 2,)),
             dma((2, 2)),
             dma((2, 2)),
-            dma,
-            dma,
+            dma((2,)),
+            dma((2,)),
             dma((32,)),
             dma((32,)),
             dma,

time: 76.4 us -> 74.7 us (0.978)
  Pallas kernels: 76.3 us -> 74.5 us
    pallas_call x1, Pallas kernels: 71.8 us -> 70.1 us  [body(): pl.pallas_call(detect_kernel, name='detect', out_shape=jax.ShapeDtypeStru...]
where the time goes in v4:
time: 74.7 us; the launch traced here: 74.5 us
  Pallas kernels  74.5 us (100%)
    pallas_call x1, Pallas kernels, body(): pl.pallas_call(detect_kernel, name='detect', out_shape=jax.ShapeDtypeStru...  70.1 us
    pallas_call x1, Pallas kernels, body(): pl.pallas_call(assemble_kernel, name='assemble', grid=(4,), out_shape=jax...  4.44 us

profile of v4, /device:TPU:1, one launch (start us, length us, event | category | flops | bytes accessed | tf_op | source)
XLA Modules:
  0.0 74.5 jit_solution(5842276489122046044)
XLA Ops:
  0.0 70.1 %detect.1.arrived = bf16[32,16,896]{2,1,0:T(8,128)(2,1)} custom-call(bf16[2,32,2,512,128]{4,3,2,1,0:T(8,128)(2,1)} %channel.1, bf16[2,32,14,2,512]{4,3,2,1,0:T(2,128)(2,1)} %bitcast.5, f32[2]{0:T(128)} %noise.1, s32[2,2]{1,0:T(2,128)} %counts.1, s32[2,1,128]{2,1,0:T(1,128)} %bitcast.6), custom_call_target="tpu_custom_call" | custom-call | tf_op jit(solution)/shard_map/detect/pallas_call | solution.py:543
  70.1 4.4 %assemble.1 = bf16[16,14,2,1024]{3,2,1,0:T(2,128)(2,1)} custom-call(bf16[32,16,896]{2,1,0:T(8,128)(2,1)} %detect.1.arrived), custom_call_target="tpu_custom_call" | custom-call | tf_op jit(solution)/shard_map/assemble/pallas_call | solution.py:605
